TPU v7x, 512 devices: a whole 4x4x16 slice. The times are simulated.
512 devices in a mesh: expert: 32 (over x, y, core), tensor: 16 (over z).
Axes of the slice: x: 4, y: 4, z: 16, core: 2. Of those that a mesh axis runs over, the one named last changes fastest.
Arguments:
- tokens: bfloat16 [1024, 7168], P('expert', 'tensor'), may hold values from -6 to 6
- expert_ids: int32 [1024, 8], P('expert'), may hold values from 0 to 31, all different within a row; in each aligned block of 32 rows (0 to 31, 32 to 63, ...) at most 24 rows name the same one
- combine: float32 [1024, 8], P('expert'), may hold values from 0.1 to 0.5
- w_in: bfloat16 [32, 7168, 2048], P('expert', None, 'tensor'), may hold values from -0.0625 to 0.0625
- w_down: bfloat16 [32, 1024, 7168], P('expert', None, 'tensor'), may hold values from -0.1875 to 0.1875
Outputs:
- moe_out: bfloat16 [1024, 7168], P('expert', 'tensor')
Inputs may be any that keep to these rules, and one draw needn't show every extreme that they name: `expert_ids`: each row names 8 different experts. Within the 32 tokens of one index of expert, no expert is named by more than 24 rows.
All inputs are finite; a program needn't handle non-finite values.
Results may differ from a plain program's by a relative error of at most 0.008.
Values may be sent and summed in bfloat16 or wider, within the bound.
No kernel may reach another device: no remote copies, remote signals or barrier semaphores. Data moves between devices by JAX's collectives and lax.ppermute only.
A program may use at most 64 MiB of HBM per device.

v0:
```python
import jax
import jax.numpy as jnp
from jax import lax
from jax.experimental import pallas as pl
from jax.experimental.pallas import tpu as pltpu
from jax.sharding import Mesh, PartitionSpec as P


XY = ("x", "y")
PAD = 128
HOPS = (0, 7, 1, 6, 2, 5, 3, 4)


def gate_up_kernel(half_ref, rows_ref, wa0_ref, wb0_ref, wa1_ref, wb1_ref, out_ref, acc_ref):
    step = pl.program_id(0)

    @pl.when(step == 0)
    def _():
        acc_ref[...] = jnp.zeros_like(acc_ref)

    weights = jnp.concatenate([wa0_ref[...], wa1_ref[...], wb0_ref[...], wb1_ref[...]], axis=1)
    acc_ref[...] += jnp.dot(rows_ref[...], weights, preferred_element_type=jnp.float32)

    @pl.when(step == pl.num_programs(0) - 1)
    def _():
        lane = lax.broadcasted_iota(jnp.int32, (rows_ref.shape[0], 128), 1)
        low = lane < 64
        first = jnp.where(low, 0, 1) == half_ref[0]

        def hidden(at):
            value = acc_ref[:, at : at + 128]
            turned = pltpu.roll(value, 64, 1)
            gate = jnp.where(low, value, turned)
            up = jnp.where(low, turned, value)
            return gate / (1.0 + jnp.exp(-gate)) * up

        for e in range(2):
            both = jnp.where(first, hidden(256 * e), hidden(256 * e + 128))
            out_ref[:, 128 * e : 128 * e + 128] = both.astype(jnp.bfloat16)


def gate_up(half, rows, wa0, wb0, wa1, wb1, depth):
    count, chunk = rows.shape[0], 1024
    w_spec = pl.BlockSpec((chunk, 128), lambda k: (k, 0))
    return pl.pallas_call(
        gate_up_kernel,
        grid=(depth // chunk,),
        in_specs=[
            pl.BlockSpec(memory_space=pltpu.SMEM),
            pl.BlockSpec((count, chunk), lambda k: (0, k)),
            w_spec,
            w_spec,
            w_spec,
            w_spec,
        ],
        out_specs=pl.BlockSpec((count, 256), lambda k: (0, 0)),
        out_shape=jax.ShapeDtypeStruct((count, 256), jnp.bfloat16),
        scratch_shapes=[pltpu.VMEM((count, 512), jnp.float32)],
        name="gate_up",
    )(half, rows, wa0, wb0, wa1, wb1)


def down_kernel(place_ref, h0, h1, h2, h3, h4, h5, h6, h7, tail_ref, da0_ref, db0_ref, da1_ref, db1_ref, out_ref):
    tail = tail_ref[...].astype(jnp.float32)
    parts = (h0, h1, h2, h3, h4, h5, h6, h7)
    weight, hidden = [], []
    for e in range(2):
        weight.append(tail[:, 3 * e : 3 * e + 1] + tail[:, 3 * e + 1 : 3 * e + 2] + tail[:, 3 * e + 2 : 3 * e + 3])
        hidden.append(jnp.concatenate([part[:, 128 * e : 128 * e + 128] for part in parts], axis=1))

    def rolled(d_ref):
        starts = [pl.multiple_of(lax.rem(place_ref[1] + by, 8) * 128, 128) for by in HOPS]
        return jnp.concatenate([d_ref[:, pl.ds(start, 128)] for start in starts], axis=1)

    for side, (a_ref, b_ref) in enumerate(((da0_ref, db0_ref), (da1_ref, db1_ref))):
        total = 0.0
        for e, d_ref in enumerate((a_ref, b_ref)):
            y = lax.dot_general(hidden[e], rolled(d_ref), (((1,), (1,)), ((), ())), preferred_element_type=jnp.float32)
            total = total + weight[e] * y.astype(jnp.bfloat16).astype(jnp.float32)
        where = place_ref[0] if side == 0 else 1 - place_ref[0]
        out_ref[where] = total.astype(jnp.bfloat16)


def down(place, parts, tail, da0, db0, da1, db1):
    count, width = parts[0].shape[0], da0.shape[0]
    vmem = pl.BlockSpec(memory_space=pltpu.VMEM)
    return pl.pallas_call(
        down_kernel,
        in_specs=[pl.BlockSpec(memory_space=pltpu.SMEM)] + [vmem] * 13,
        out_specs=vmem,
        out_shape=jax.ShapeDtypeStruct((2, count, width), jnp.bfloat16),
        name="down",
    )(place, *parts, tail, da0, db0, da1, db1)


def ring_gather(shard):
    left = tuple((j, (j + 1) % 8) for j in range(8))
    right = tuple((j, (j - 1) % 8) for j in range(8))
    parts, ahead, behind = [shard], shard, shard
    for step in range(4):
        ahead = lax.ppermute(ahead, "zh", left)
        parts.append(ahead)
        if step < 3:
            behind = lax.ppermute(behind, "zh", right)
            parts.append(behind)
    return parts


def combine_tail(ids, comb, core, half):
    rows, experts = ids.shape[0] // 2, 32
    ids = jnp.where(half == 0, ids[:rows], ids[rows:])
    comb = jnp.where(half == 0, comb[:rows], comb[rows:])
    hit = ids[:, :, None] == jnp.arange(experts, dtype=jnp.int32)[None, None, :]
    dense = jnp.sum(jnp.where(hit, comb[:, :, None], 0.0), axis=1)
    dense = jnp.transpose(dense.reshape(rows, experts // 2, 2), (1, 0, 2))
    pair = jnp.where(core == 0, dense, dense[:, :, ::-1])
    high = lax.reduce_precision(pair, 8, 7)
    middle = lax.reduce_precision(pair - high, 8, 7)
    low = lax.reduce_precision(pair - high - middle, 8, 7)
    pieces = jnp.stack([high, middle, low], axis=3).reshape(experts // 2, rows, 6)
    return jnp.pad(pieces.astype(jnp.bfloat16), ((0, 0), (0, 0), (0, PAD - 6)))


def layer(tokens, ids, comb, w_in, w_down):
    core, half = lax.axis_index("c"), lax.axis_index("zl")
    place = jnp.stack([half, lax.axis_index("zh")]).astype(jnp.int32)
    swap = ((0, 1), (1, 0))
    w_in, w_down = w_in[0], w_down[0].T
    rows, feats = tokens.shape[0] // 2, tokens.shape[1]
    depth = w_in.shape[0]

    wa0, da0 = w_in, w_down
    wb0 = lax.ppermute(w_in, "c", swap)
    db0 = lax.ppermute(w_down, "c", swap)
    wa1 = lax.ppermute(w_in, "zl", swap)
    da1 = lax.ppermute(w_down, "zl", swap)
    wb1 = lax.ppermute(wa1, "c", swap)
    db1 = lax.ppermute(da1, "c", swap)

    pieces = jnp.broadcast_to(tokens.reshape(1, 2, rows, feats), (8, 2, rows, feats))
    pieces = lax.all_to_all(pieces.reshape(16, rows, feats), ("zh", "zl"), 0, 0, tiled=True)
    whole = jnp.transpose(pieces, (1, 0, 2)).reshape(rows, depth)
    tail = combine_tail(ids, comb, core, half)
    sent = jnp.concatenate([jnp.broadcast_to(whole[None], (16, rows, depth)), tail], axis=2)
    got = lax.all_to_all(sent, XY, 0, 0, tiled=True).reshape(16 * rows, depth + PAD)
    hidden = gate_up(place, got, wa0, wb0, wa1, wb1, depth)
    parts = ring_gather(hidden)
    out = down(place, parts, got[:, depth:], da0, db0, da1, db1)
    back = lax.all_to_all(out.reshape(32, rows, feats), ("zl",) + XY, 0, 0, tiled=True)
    total = jnp.sum(back.reshape(2, 16, rows, feats).astype(jnp.float32), axis=1)
    return total.reshape(2 * rows, feats).astype(jnp.bfloat16)


def solution(mesh):
    fine = Mesh(mesh.devices.reshape(4, 4, 2, 8, 2), ("x", "y", "c", "zh", "zl"))
    e, t = ("x", "y", "c"), ("zh", "zl")
    in_specs = (P(e, t), P(e, None), P(e, None), P(e, None, t), P(e, None, t))
    return jax.shard_map(layer, mesh=fine, in_specs=in_specs, out_specs=P(e, t), check_vma=False)
```

profile of v0, /device:TPU:1, one launch (start us, length us, event | category | flops | bytes accessed | tf_op | source)
XLA Modules:
  0.0 174.5 jit_solution(16330426594928050011)
XLA Ops:
  0.0 1.5 broadcast_in_dim.30
  1.5 15.7 %all-to-all-start = ((bf16[16,16,448]{2,1,0:T(8,128)(2,1)}), bf16[16,16,448]{2,1,0:T(8,128)(2,1)S(1)}, u32[]{:S(2)}, u32[]{:S(2)}) async-start(bf16[16,16,448]{2,1,0:T(8,128)(2,1)} %bitcast.3), calls=%async_computation | async-start | bytes 524288 | tf_op jit(solution)/shard_map/all_to_all | solution.py:141
  17.2 3.3 %collective-permute-start.1 = (bf16[7168,128]{1,0:T(8,128)(2,1)}, bf16[7168,128]{1,0:T(8,128)(2,1)}, u32[]{:S(2)}, u32[]{:S(2)}) collective-permute-start(bf16[7168,128]{1,0:T(8,128)(2,1)} %bitcast.28), channel_id=1, source_target_pairs={{0,1},{1,0},{2,3},{3,2},{4,5},{5,4},{6,7},{7,6},{8,9},{9,8},{10,11... | collective-permute-start | bytes 5505032 | tf_op jit(solution)/shard_map/ppermute | solution.py:135
  20.5 0.8 slice_select_fusion.1
  21.3 0.1 copy.40
  21.4 0.8 slice_select_fusion
  22.2 0.1 copy.41
  22.3 0.1 select_reduce_fusion
  22.4 0.1 copy.42
  22.6 0.2 copy.47
  22.8 8.2 %all-to-all-done = bf16[16,16,448]{2,1,0:T(8,128)(2,1)S(1)} async-done(((bf16[16,16,448]{2,1,0:T(8,128)(2,1)}), bf16[16,16,448]{2,1,0:T(8,128)(2,1)S(1)}, u32[]{:S(2)}, u32[]{:S(2)}) %all-to-all-start) | async-done | bytes 229408 | tf_op jit(solution)/shard_map/all_to_all | solution.py:141
  31.0 0.1 copy.39
  31.1 0.3 broadcast_in_dim.31
  31.4 0.4 broadcast_in_dim.32
  31.8 2.1 %fusion.1 = bf16[16,16,7296]{2,1,0:T(8,128)(2,1)} fusion(bf16[16,16,6]{2,1,0:T(8,128)(2,1)S(1)} %copy.47, bf16[16,16,7168]{2,1,0:T(8,128)(2,1)S(1)} %broadcast_in_dim.32), kind=kLoop, calls=%fused_computation.2 | loop fusion | flops 11206656 | bytes 7408640 | tf_op jit(solution)/shard_map/concatenate | solution.py:144
  34.0 0.0 copy-start
  34.0 0.0 copy-start.1
  34.0 7.1 %all-to-all-start.1 = ((bf16[16,16,7296]{2,1,0:T(8,128)(2,1)}), bf16[16,16,7296]{2,1,0:T(8,128)(2,1)}, u32[]{:S(2)}, u32[]{:S(2)}) async-start(bf16[16,16,7296]{2,1,0:T(8,128)(2,1)} %fusion.1), calls=%async_computation.1 | async-start | bytes 7471104 | tf_op jit(solution)/shard_map/all_to_all | solution.py:145
  41.0 0.0 copy-done
  41.1 7.8 %collective-permute-start = (bf16[7168,128]{1,0:T(8,128)(2,1)S(1)}, bf16[7168,128]{1,0:T(8,128)(2,1)}, u32[]{:S(2)}, u32[]{:S(2)}) collective-permute-start(bf16[7168,128]{1,0:T(8,128)(2,1)S(1)} %bitcast.30), channel_id=1, source_target_pairs={{0,16},{16,0},{1,17},{17,1},{2,18},{18,2},{3,19},{19,3},{4,20},{20... | collective-permute-start | bytes 5505032 | tf_op jit(solution)/shard_map/ppermute | solution.py:133
  48.8 20.9 %collective-permute-done.1.wa1_ref = bf16[7168,128]{1,0:T(8,128)(2,1)} collective-permute-done((bf16[7168,128]{1,0:T(8,128)(2,1)}, bf16[7168,128]{1,0:T(8,128)(2,1)}, u32[]{:S(2)}, u32[]{:S(2)}) %collective-permute-start.1) | collective-permute-done | bytes 1835040 | tf_op jit(solution)/shard_map/ppermute | solution.py:135
  69.7 3.3 %collective-permute-start.2 = (bf16[7168,128]{1,0:T(8,128)(2,1)}, bf16[7168,128]{1,0:T(8,128)(2,1)}, u32[]{:S(2)}, u32[]{:S(2)}) collective-permute-start(bf16[7168,128]{1,0:T(8,128)(2,1)} %collective-permute-done.1.wa1_ref), channel_id=1, source_target_pairs={{0,16},{16,0},{1,17},{17,1},{2,18},{18,2},{3,19},{19,3},{4,20},{20... | collective-permute-start | bytes 5505032 | tf_op jit(solution)/shard_map/ppermute | solution.py:137
  73.0 0.0 copy-done.1
  73.1 1.9 %collective-permute-start.11 = (bf16[448,1024]{1,0:T(8,128)(2,1)S(1)}, bf16[448,1024]{1,0:T(8,128)(2,1)}, u32[]{:S(2)}, u32[]{:S(2)}) collective-permute-start(bf16[448,1024]{1,0:T(8,128)(2,1)S(1)} %bitcast.33), channel_id=1, source_target_pairs={{0,1},{1,0},{2,3},{3,2},{4,5},{5,4},{6,7},{7,6},{8,9},{9,8},{10,11... | collective-permute-start | bytes 2752520 | tf_op jit(solution)/shard_map/ppermute | solution.py:136
  75.0 2.1 %collective-permute-start.10 = (bf16[448,1024]{1,0:T(8,128)(2,1)S(1)}, bf16[448,1024]{1,0:T(8,128)(2,1)}, u32[]{:S(2)}, u32[]{:S(2)}) collective-permute-start(bf16[448,1024]{1,0:T(8,128)(2,1)S(1)} %bitcast.34), channel_id=1, source_target_pairs={{0,16},{16,0},{1,17},{17,1},{2,18},{18,2},{3,19},{19,3},{4,20},{20... | collective-permute-start | bytes 2752520 | tf_op jit(solution)/shard_map/ppermute | solution.py:134
  77.1 19.8 %collective-permute-done.11.da1_ref = bf16[448,1024]{1,0:T(8,128)(2,1)} collective-permute-done((bf16[448,1024]{1,0:T(8,128)(2,1)S(1)}, bf16[448,1024]{1,0:T(8,128)(2,1)}, u32[]{:S(2)}, u32[]{:S(2)}) %collective-permute-start.11) | collective-permute-done | bytes 917536 | tf_op jit(solution)/shard_map/ppermute | solution.py:136
  96.9 2.8 %collective-permute-start.12 = (bf16[448,1024]{1,0:T(8,128)(2,1)}, bf16[448,1024]{1,0:T(8,128)(2,1)}, u32[]{:S(2)}, u32[]{:S(2)}) collective-permute-start(bf16[448,1024]{1,0:T(8,128)(2,1)} %collective-permute-done.11.da1_ref), channel_id=1, source_target_pairs={{0,16},{16,0},{1,17},{17,1},{2,18},{18,2},{3,19},{19,3},{4,20},{20... | collective-permute-start | bytes 2752520 | tf_op jit(solution)/shard_map/ppermute | solution.py:138
  99.7 0.7 pad_add_fusion.half_ref.place_ref
  100.4 0.0 collective-permute-done.wb0_ref
  100.4 0.0 collective-permute-done.2.wb1_ref
  100.4 0.0 all-to-all-done.1
  100.4 8.3 %gate_up.1.h0 = bf16[256,256]{1,0:T(8,128)(2,1)} custom-call(s32[2]{0:T(128)} %pad_add_fusion.half_ref.place_ref, bf16[256,7296]{1,0:T(8,128)(2,1)} %bitcast.12.rows_ref, bf16[7168,128]{1,0:T(8,128)(2,1)} %bitcast.29, bf16[7168,128]{1,0:T(8,128)(2,1)} %collective-permute-done.wb0_ref, bf16[7168,128]{1,0:T(8,128)(2,1)} %collective-permute-done.1.wa1_ref, ...), custom_call_target="tpu_custom_call" | custom-call | tf_op jit(solution)/shard_map/gate_up/pallas_call | solution.py:45
  108.7 4.1 %collective-permute-start.3 = (bf16[256,256]{1,0:T(8,128)(2,1)}, bf16[256,256]{1,0:T(8,128)(2,1)S(1)}, u32[]{:S(2)}, u32[]{:S(2)}) collective-permute-start(bf16[256,256]{1,0:T(8,128)(2,1)} %gate_up.1.h0), channel_id=1, source_target_pairs={{0,2},{2,4},{4,6},{6,8},{8,10},{10,12},{12,14},{14,0},{1,3},{3,5},... | collective-permute-start | bytes 393224 | tf_op jit(solution)/shard_map/ppermute | solution.py:101
  112.8 3.3 %collective-permute-start.4 = (bf16[256,256]{1,0:T(8,128)(2,1)}, bf16[256,256]{1,0:T(8,128)(2,1)S(1)}, u32[]{:S(2)}, u32[]{:S(2)}) collective-permute-start(bf16[256,256]{1,0:T(8,128)(2,1)} %gate_up.1.h0), channel_id=1, source_target_pairs={{0,14},{2,0},{4,2},{6,4},{8,6},{10,8},{12,10},{14,12},{1,15},{3,1}... | collective-permute-start | bytes 393224 | tf_op jit(solution)/shard_map/ppermute | solution.py:104
  116.1 2.0 %collective-permute-done.3.h1 = bf16[256,256]{1,0:T(8,128)(2,1)S(1)} collective-permute-done((bf16[256,256]{1,0:T(8,128)(2,1)}, bf16[256,256]{1,0:T(8,128)(2,1)S(1)}, u32[]{:S(2)}, u32[]{:S(2)}) %collective-permute-start.3) | collective-permute-done | bytes 131104 | tf_op jit(solution)/shard_map/ppermute | solution.py:101
  118.1 0.0 copy-start.2
  118.1 4.5 %collective-permute-start.5 = (bf16[256,256]{1,0:T(8,128)(2,1)S(1)}, bf16[256,256]{1,0:T(8,128)(2,1)S(1)}, u32[]{:S(2)}, u32[]{:S(2)}) collective-permute-start(bf16[256,256]{1,0:T(8,128)(2,1)S(1)} %collective-permute-done.3.h1), channel_id=1, source_target_pairs={{0,2},{2,4},{4,6},{6,8},{8,10},{10,12},{12,14},{14,0},{1,3},{3,5},... | collective-permute-start | bytes 393224 | tf_op jit(solution)/shard_map/ppermute | solution.py:101
  122.5 2.2 %collective-permute-done.4.h2 = bf16[256,256]{1,0:T(8,128)(2,1)S(1)} collective-permute-done((bf16[256,256]{1,0:T(8,128)(2,1)}, bf16[256,256]{1,0:T(8,128)(2,1)S(1)}, u32[]{:S(2)}, u32[]{:S(2)}) %collective-permute-start.4) | collective-permute-done | bytes 131104 | tf_op jit(solution)/shard_map/ppermute | solution.py:104
  124.7 0.0 copy-start.3
  124.7 3.5 %collective-permute-start.6 = (bf16[256,256]{1,0:T(8,128)(2,1)S(1)}, bf16[256,256]{1,0:T(8,128)(2,1)S(1)}, u32[]{:S(2)}, u32[]{:S(2)}) collective-permute-start(bf16[256,256]{1,0:T(8,128)(2,1)S(1)} %collective-permute-done.4.h2), channel_id=1, source_target_pairs={{0,14},{2,0},{4,2},{6,4},{8,6},{10,8},{12,10},{14,12},{1,15},{3,1}... | collective-permute-start | bytes 393224 | tf_op jit(solution)/shard_map/ppermute | solution.py:104
  128.3 0.0 collective-permute-done.5.h3
  128.3 0.0 copy-start.4
  128.3 3.8 %collective-permute-start.7 = (bf16[256,256]{1,0:T(8,128)(2,1)S(1)}, bf16[256,256]{1,0:T(8,128)(2,1)S(1)}, u32[]{:S(2)}, u32[]{:S(2)}) collective-permute-start(bf16[256,256]{1,0:T(8,128)(2,1)S(1)} %collective-permute-done.5.h3), channel_id=1, source_target_pairs={{0,2},{2,4},{4,6},{6,8},{8,10},{10,12},{12,14},{14,0},{1,3},{3,5},... | collective-permute-start | bytes 393224 | tf_op jit(solution)/shard_map/ppermute | solution.py:101
  132.1 4.5 %collective-permute-done.6.h4 = bf16[256,256]{1,0:T(8,128)(2,1)S(1)} collective-permute-done((bf16[256,256]{1,0:T(8,128)(2,1)S(1)}, bf16[256,256]{1,0:T(8,128)(2,1)S(1)}, u32[]{:S(2)}, u32[]{:S(2)}) %collective-permute-start.6) | collective-permute-done | bytes 131104 | tf_op jit(solution)/shard_map/ppermute | solution.py:104
  136.6 3.5 %collective-permute-start.8 = (bf16[256,256]{1,0:T(8,128)(2,1)S(1)}, bf16[256,256]{1,0:T(8,128)(2,1)S(1)}, u32[]{:S(2)}, u32[]{:S(2)}) collective-permute-start(bf16[256,256]{1,0:T(8,128)(2,1)S(1)} %collective-permute-done.6.h4), channel_id=1, source_target_pairs={{0,14},{2,0},{4,2},{6,4},{8,6},{10,8},{12,10},{14,12},{1,15},{3,1}... | collective-permute-start | bytes 393224 | tf_op jit(solution)/shard_map/ppermute | solution.py:104
  140.1 0.0 collective-permute-done.7.h5
  140.1 0.0 copy-start.6
  140.1 2.8 %collective-permute-start.9 = (bf16[256,256]{1,0:T(8,128)(2,1)S(1)}, bf16[256,256]{1,0:T(8,128)(2,1)S(1)}, u32[]{:S(2)}, u32[]{:S(2)}) collective-permute-start(bf16[256,256]{1,0:T(8,128)(2,1)S(1)} %collective-permute-done.7.h5), channel_id=1, source_target_pairs={{0,2},{2,4},{4,6},{6,8},{8,10},{10,12},{12,14},{14,0},{1,3},{3,5},... | collective-permute-start | bytes 393224 | tf_op jit(solution)/shard_map/ppermute | solution.py:101
  143.0 1.5 slice.20.tail_ref
  144.4 0.0 collective-permute-done.10.db0_ref
  144.4 0.0 collective-permute-done.12.db1_ref
  144.4 2.0 %collective-permute-done.8.h6 = bf16[256,256]{1,0:T(8,128)(2,1)S(1)} collective-permute-done((bf16[256,256]{1,0:T(8,128)(2,1)S(1)}, bf16[256,256]{1,0:T(8,128)(2,1)S(1)}, u32[]{:S(2)}, u32[]{:S(2)}) %collective-permute-start.8) | collective-permute-done | bytes 131104 | tf_op jit(solution)/shard_map/ppermute | solution.py:104
  146.5 5.4 %collective-permute-done.9.h7 = bf16[256,256]{1,0:T(8,128)(2,1)S(1)} collective-permute-done((bf16[256,256]{1,0:T(8,128)(2,1)S(1)}, bf16[256,256]{1,0:T(8,128)(2,1)S(1)}, u32[]{:S(2)}, u32[]{:S(2)}) %collective-permute-start.9) | collective-permute-done | bytes 131104 | tf_op jit(solution)/shard_map/ppermute | solution.py:101
  151.9 0.0 copy-done.2
  151.9 0.0 copy-done.3
  151.9 0.0 copy-done.4
  151.9 0.0 copy-done.5
  151.9 0.0 copy-done.6
  151.9 0.0 copy-done.7
  151.9 0.0 copy-start.8
  151.9 0.6 copy-done.8
  152.6 4.7 %down.1 = bf16[2,256,448]{2,1,0:T(8,128)(2,1)} custom-call(s32[2]{0:T(128)} %pad_add_fusion.half_ref.place_ref, bf16[256,256]{1,0:T(8,128)(2,1)} %gate_up.1.h0, bf16[256,256]{1,0:T(8,128)(2,1)} %copy-done.2, bf16[256,256]{1,0:T(8,128)(2,1)} %copy-done.3, bf16[256,256]{1,0:T(8,128)(2,1)} %copy-done.4, bf16[256,256]{1,0:T(8,128)(2,1)} %copy-done.5, ...), custom_call_target="tpu_custom_call" | custom-call | tf_op jit(solution)/shard_map/down/pallas_call | solution.py:87
  157.2 16.6 %all_to_all.15 = bf16[32,16,448]{2,1,0:T(8,128)(2,1)S(1)} all-to-all(bf16[32,16,448]{2,1,0:T(8,128)(2,1)} %bitcast.27), channel_id=1, replica_groups=mesh['x'=4,'y'=4,'c'=2,'zh'=8,'zl'=2] {'zl','x','y'}, dimensions={0} | all-to-all | bytes 917504 | tf_op jit(solution)/shard_map/all_to_all | solution.py:149
  173.8 0.7 bitcast_reduce_fusion
  (6 shorter events, 0.0 us)
Async XLA Ops:
  1.5 29.5 %all-to-all-start = ((bf16[16,16,448]{2,1,0:T(8,128)(2,1)}), bf16[16,16,448]{2,1,0:T(8,128)(2,1)S(1)}, u32[]{:S(2)}, u32[]{:S(2)}) async-start(bf16[16,16,448]{2,1,0:T(8,128)(2,1)} %bitcast.3), calls=%async_computation | async-start | bytes 524288 | tf_op jit(solution)/shard_map/all_to_all | solution.py:141
  17.2 52.5 %collective-permute-start.1 = (bf16[7168,128]{1,0:T(8,128)(2,1)}, bf16[7168,128]{1,0:T(8,128)(2,1)}, u32[]{:S(2)}, u32[]{:S(2)}) collective-permute-start(bf16[7168,128]{1,0:T(8,128)(2,1)} %bitcast.28), channel_id=1, source_target_pairs={{0,1},{1,0},{2,3},{3,2},{4,5},{5,4},{6,7},{7,6},{8,9},{9,8},{10,11... | collective-permute-start | bytes 5505032 | tf_op jit(solution)/shard_map/ppermute | solution.py:135
  34.0 7.1 %copy-start = (bf16[1,7168,128]{2,1,0:T(8,128)(2,1)S(1)}, bf16[1,7168,128]{2,1,0:T(8,128)(2,1)}, u32[]{:S(2)}) copy-start(bf16[1,7168,128]{2,1,0:T(8,128)(2,1)} %param.8) | copy-start | bytes 5505028
  34.0 39.1 %copy-start.1 = (bf16[1,1024,448]{1,2,0:T(8,128)(2,1)S(1)}, bf16[1,1024,448]{1,2,0:T(8,128)(2,1)}, u32[]{:S(2)}) copy-start(bf16[1,1024,448]{1,2,0:T(8,128)(2,1)} %param.9) | copy-start | bytes 2752516
  34.0 66.4 %all-to-all-start.1 = ((bf16[16,16,7296]{2,1,0:T(8,128)(2,1)}), bf16[16,16,7296]{2,1,0:T(8,128)(2,1)}, u32[]{:S(2)}, u32[]{:S(2)}) async-start(bf16[16,16,7296]{2,1,0:T(8,128)(2,1)} %fusion.1), calls=%async_computation.1 | async-start | bytes 7471104 | tf_op jit(solution)/shard_map/all_to_all | solution.py:145
  41.1 59.3 %collective-permute-start = (bf16[7168,128]{1,0:T(8,128)(2,1)S(1)}, bf16[7168,128]{1,0:T(8,128)(2,1)}, u32[]{:S(2)}, u32[]{:S(2)}) collective-permute-start(bf16[7168,128]{1,0:T(8,128)(2,1)S(1)} %bitcast.30), channel_id=1, source_target_pairs={{0,16},{16,0},{1,17},{17,1},{2,18},{18,2},{3,19},{19,3},{4,20},{20... | collective-permute-start | bytes 5505032 | tf_op jit(solution)/shard_map/ppermute | solution.py:133
  69.7 30.7 %collective-permute-start.2 = (bf16[7168,128]{1,0:T(8,128)(2,1)}, bf16[7168,128]{1,0:T(8,128)(2,1)}, u32[]{:S(2)}, u32[]{:S(2)}) collective-permute-start(bf16[7168,128]{1,0:T(8,128)(2,1)} %collective-permute-done.1.wa1_ref), channel_id=1, source_target_pairs={{0,16},{16,0},{1,17},{17,1},{2,18},{18,2},{3,19},{19,3},{4,20},{20... | collective-permute-start | bytes 5505032 | tf_op jit(solution)/shard_map/ppermute | solution.py:137
  73.1 23.9 %collective-permute-start.11 = (bf16[448,1024]{1,0:T(8,128)(2,1)S(1)}, bf16[448,1024]{1,0:T(8,128)(2,1)}, u32[]{:S(2)}, u32[]{:S(2)}) collective-permute-start(bf16[448,1024]{1,0:T(8,128)(2,1)S(1)} %bitcast.33), channel_id=1, source_target_pairs={{0,1},{1,0},{2,3},{3,2},{4,5},{5,4},{6,7},{7,6},{8,9},{9,8},{10,11... | collective-permute-start | bytes 2752520 | tf_op jit(solution)/shard_map/ppermute | solution.py:136
  75.0 69.4 %collective-permute-start.10 = (bf16[448,1024]{1,0:T(8,128)(2,1)S(1)}, bf16[448,1024]{1,0:T(8,128)(2,1)}, u32[]{:S(2)}, u32[]{:S(2)}) collective-permute-start(bf16[448,1024]{1,0:T(8,128)(2,1)S(1)} %bitcast.34), channel_id=1, source_target_pairs={{0,16},{16,0},{1,17},{17,1},{2,18},{18,2},{3,19},{19,3},{4,20},{20... | collective-permute-start | bytes 2752520 | tf_op jit(solution)/shard_map/ppermute | solution.py:134
  96.9 47.5 %collective-permute-start.12 = (bf16[448,1024]{1,0:T(8,128)(2,1)}, bf16[448,1024]{1,0:T(8,128)(2,1)}, u32[]{:S(2)}, u32[]{:S(2)}) collective-permute-start(bf16[448,1024]{1,0:T(8,128)(2,1)} %collective-permute-done.11.da1_ref), channel_id=1, source_target_pairs={{0,16},{16,0},{1,17},{17,1},{2,18},{18,2},{3,19},{19,3},{4,20},{20... | collective-permute-start | bytes 2752520 | tf_op jit(solution)/shard_map/ppermute | solution.py:138
  108.7 9.4 %collective-permute-start.3 = (bf16[256,256]{1,0:T(8,128)(2,1)}, bf16[256,256]{1,0:T(8,128)(2,1)S(1)}, u32[]{:S(2)}, u32[]{:S(2)}) collective-permute-start(bf16[256,256]{1,0:T(8,128)(2,1)} %gate_up.1.h0), channel_id=1, source_target_pairs={{0,2},{2,4},{4,6},{6,8},{8,10},{10,12},{12,14},{14,0},{1,3},{3,5},... | collective-permute-start | bytes 393224 | tf_op jit(solution)/shard_map/ppermute | solution.py:101
  112.8 12.0 %collective-permute-start.4 = (bf16[256,256]{1,0:T(8,128)(2,1)}, bf16[256,256]{1,0:T(8,128)(2,1)S(1)}, u32[]{:S(2)}, u32[]{:S(2)}) collective-permute-start(bf16[256,256]{1,0:T(8,128)(2,1)} %gate_up.1.h0), channel_id=1, source_target_pairs={{0,14},{2,0},{4,2},{6,4},{8,6},{10,8},{12,10},{14,12},{1,15},{3,1}... | collective-permute-start | bytes 393224 | tf_op jit(solution)/shard_map/ppermute | solution.py:104
  118.1 33.8 %copy-start.2 = (bf16[256,256]{1,0:T(8,128)(2,1)}, bf16[256,256]{1,0:T(8,128)(2,1)S(1)}, u32[]{:S(2)}) copy-start(bf16[256,256]{1,0:T(8,128)(2,1)S(1)} %collective-permute-done.3.h1) | copy-start | bytes 393220
  118.1 10.2 %collective-permute-start.5 = (bf16[256,256]{1,0:T(8,128)(2,1)S(1)}, bf16[256,256]{1,0:T(8,128)(2,1)S(1)}, u32[]{:S(2)}, u32[]{:S(2)}) collective-permute-start(bf16[256,256]{1,0:T(8,128)(2,1)S(1)} %collective-permute-done.3.h1), channel_id=1, source_target_pairs={{0,2},{2,4},{4,6},{6,8},{8,10},{10,12},{12,14},{14,0},{1,3},{3,5},... | collective-permute-start | bytes 393224 | tf_op jit(solution)/shard_map/ppermute | solution.py:101
  124.7 27.1 %copy-start.3 = (bf16[256,256]{1,0:T(8,128)(2,1)}, bf16[256,256]{1,0:T(8,128)(2,1)S(1)}, u32[]{:S(2)}) copy-start(bf16[256,256]{1,0:T(8,128)(2,1)S(1)} %collective-permute-done.4.h2) | copy-start | bytes 393220
  124.7 11.9 %collective-permute-start.6 = (bf16[256,256]{1,0:T(8,128)(2,1)S(1)}, bf16[256,256]{1,0:T(8,128)(2,1)S(1)}, u32[]{:S(2)}, u32[]{:S(2)}) collective-permute-start(bf16[256,256]{1,0:T(8,128)(2,1)S(1)} %collective-permute-done.4.h2), channel_id=1, source_target_pairs={{0,14},{2,0},{4,2},{6,4},{8,6},{10,8},{12,10},{14,12},{1,15},{3,1}... | collective-permute-start | bytes 393224 | tf_op jit(solution)/shard_map/ppermute | solution.py:104
  128.3 23.6 %copy-start.4 = (bf16[256,256]{1,0:T(8,128)(2,1)}, bf16[256,256]{1,0:T(8,128)(2,1)S(1)}, u32[]{:S(2)}) copy-start(bf16[256,256]{1,0:T(8,128)(2,1)S(1)} %collective-permute-done.5.h3) | copy-start | bytes 393220
  128.3 11.8 %collective-permute-start.7 = (bf16[256,256]{1,0:T(8,128)(2,1)S(1)}, bf16[256,256]{1,0:T(8,128)(2,1)S(1)}, u32[]{:S(2)}, u32[]{:S(2)}) collective-permute-start(bf16[256,256]{1,0:T(8,128)(2,1)S(1)} %collective-permute-done.5.h3), channel_id=1, source_target_pairs={{0,2},{2,4},{4,6},{6,8},{8,10},{10,12},{12,14},{14,0},{1,3},{3,5},... | collective-permute-start | bytes 393224 | tf_op jit(solution)/shard_map/ppermute | solution.py:101
  136.6 15.3 %copy-start.5 = (bf16[256,256]{1,0:T(8,128)(2,1)}, bf16[256,256]{1,0:T(8,128)(2,1)S(1)}, u32[]{:S(2)}) copy-start(bf16[256,256]{1,0:T(8,128)(2,1)S(1)} %collective-permute-done.6.h4) | copy-start | bytes 393220
  136.6 9.9 %collective-permute-start.8 = (bf16[256,256]{1,0:T(8,128)(2,1)S(1)}, bf16[256,256]{1,0:T(8,128)(2,1)S(1)}, u32[]{:S(2)}, u32[]{:S(2)}) collective-permute-start(bf16[256,256]{1,0:T(8,128)(2,1)S(1)} %collective-permute-done.6.h4), channel_id=1, source_target_pairs={{0,14},{2,0},{4,2},{6,4},{8,6},{10,8},{12,10},{14,12},{1,15},{3,1}... | collective-permute-start | bytes 393224 | tf_op jit(solution)/shard_map/ppermute | solution.py:104
  140.1 11.8 %copy-start.6 = (bf16[256,256]{1,0:T(8,128)(2,1)}, bf16[256,256]{1,0:T(8,128)(2,1)S(1)}, u32[]{:S(2)}) copy-start(bf16[256,256]{1,0:T(8,128)(2,1)S(1)} %collective-permute-done.7.h5) | copy-start | bytes 393220
  140.1 11.7 %collective-permute-start.9 = (bf16[256,256]{1,0:T(8,128)(2,1)S(1)}, bf16[256,256]{1,0:T(8,128)(2,1)S(1)}, u32[]{:S(2)}, u32[]{:S(2)}) collective-permute-start(bf16[256,256]{1,0:T(8,128)(2,1)S(1)} %collective-permute-done.7.h5), channel_id=1, source_target_pairs={{0,2},{2,4},{4,6},{6,8},{8,10},{10,12},{12,14},{14,0},{1,3},{3,5},... | collective-permute-start | bytes 393224 | tf_op jit(solution)/shard_map/ppermute | solution.py:101
  146.5 5.4 %copy-start.7 = (bf16[256,256]{1,0:T(8,128)(2,1)}, bf16[256,256]{1,0:T(8,128)(2,1)S(1)}, u32[]{:S(2)}) copy-start(bf16[256,256]{1,0:T(8,128)(2,1)S(1)} %collective-permute-done.8.h6) | copy-start | bytes 393220
  151.9 0.7 copy-start.8
where the time goes:
time: 176 us; the launch traced here: 175 us
  starting transfers between devices  69.5 us (39%)
  waiting for transfers between devices  65.1 us (37%)
  blocking collectives  16.6 us (9%)
  Pallas kernels  12.9 us (7%)
  other arithmetic  5.29 us (3%)
  local copies, waits for them, and re-layouts  4.87 us (3%)
    ppermute x1, waiting for transfers between devices, layer(): wa1 = lax.ppermute(w_in, 'zl', swap)  20.9 us
    ppermute x1, waiting for transfers between devices, layer(): da1 = lax.ppermute(w_down, 'zl', swap)  19.8 us
    all_to_all x1, blocking collectives, layer(): lax.all_to_all(out.reshape(32, rows, feats), ('zl',) + XY, 0, 0, tiled=True)  16.6 us
    all_to_all x1, starting transfers between devices, layer(): lax.all_to_all(pieces.reshape(16, rows, feats), ('zh', 'zl'), 0, 0, tiled...  15.7 us
    ppermute x4, starting transfers between devices, ring_gather(): ahead = lax.ppermute(ahead, 'zh', left)  15.2 us
    ppermute x3, starting transfers between devices, ring_gather(): behind = lax.ppermute(behind, 'zh', right)  10.3 us
    ppermute x3, waiting for transfers between devices, ring_gather(): behind = lax.ppermute(behind, 'zh', right)  8.72 us
    pallas_call x1, Pallas kernels, gate_up(): pl.pallas_call(gate_up_kernel, grid=(depth // chunk,), in_specs=[pl.Block...  8.27 us
  transfers between devices with their start and end apart: 15, of which 8 were waited for; matrix products, arithmetic and copies ran while one was open for 4% of the time, Pallas kernels for 5%

commit v1 on v0

--- a/solution.py
+++ b/solution.py
@@ -8,10 +8,10 @@
 
 XY = ("x", "y")
 PAD = 128
-HOPS = (0, 7, 1, 6, 2, 5, 3, 4)
+MAIN = 240
 
 
-def gate_up_kernel(half_ref, rows_ref, wa0_ref, wb0_ref, wa1_ref, wb1_ref, out_ref, acc_ref):
+def gate_up_kernel(half_ref, rows_ref, wa0_ref, wb0_ref, wa1_ref, wb1_ref, main_ref, rest_ref, acc_ref):
     step = pl.program_id(0)
 
     @pl.when(step == 0)
@@ -36,7 +36,10 @@
 
         for e in range(2):
             both = jnp.where(first, hidden(256 * e), hidden(256 * e + 128))
-            out_ref[:, 128 * e : 128 * e + 128] = both.astype(jnp.bfloat16)
+            both = both.astype(jnp.bfloat16)
+            main_ref[:, 128 * e : 128 * e + 128] = both[:MAIN]
+            for j in range(rest_ref.shape[0]):
+                rest_ref[j, :, 128 * e : 128 * e + 128] = both[MAIN:]
 
 
 def gate_up(half, rows, wa0, wb0, wa1, wb1, depth):
@@ -53,57 +56,51 @@
             w_spec,
             w_spec,
         ],
-        out_specs=pl.BlockSpec((count, 256), lambda k: (0, 0)),
-        out_shape=jax.ShapeDtypeStruct((count, 256), jnp.bfloat16),
+        out_specs=(
+            pl.BlockSpec((MAIN, 256), lambda k: (0, 0)),
+            pl.BlockSpec((8, count - MAIN, 256), lambda k: (0, 0, 0)),
+        ),
+        out_shape=(
+            jax.ShapeDtypeStruct((MAIN, 256), jnp.bfloat16),
+            jax.ShapeDtypeStruct((8, count - MAIN, 256), jnp.bfloat16),
+        ),
         scratch_shapes=[pltpu.VMEM((count, 512), jnp.float32)],
         name="gate_up",
     )(half, rows, wa0, wb0, wa1, wb1)
 
 
-def down_kernel(place_ref, h0, h1, h2, h3, h4, h5, h6, h7, tail_ref, da0_ref, db0_ref, da1_ref, db1_ref, out_ref):
+def down_kernel(place_ref, main_ref, rest_ref, tail_ref, da0_ref, db0_ref, da1_ref, db1_ref, out_ref):
     tail = tail_ref[...].astype(jnp.float32)
-    parts = (h0, h1, h2, h3, h4, h5, h6, h7)
     weight, hidden = [], []
     for e in range(2):
         weight.append(tail[:, 3 * e : 3 * e + 1] + tail[:, 3 * e + 1 : 3 * e + 2] + tail[:, 3 * e + 2 : 3 * e + 3])
-        hidden.append(jnp.concatenate([part[:, 128 * e : 128 * e + 128] for part in parts], axis=1))
-
-    def rolled(d_ref):
-        starts = [pl.multiple_of(lax.rem(place_ref[1] + by, 8) * 128, 128) for by in HOPS]
-        return jnp.concatenate([d_ref[:, pl.ds(start, 128)] for start in starts], axis=1)
-
+        pieces = [
+            jnp.concatenate([ref[j, :, 128 * e : 128 * e + 128] for ref in (main_ref, rest_ref)], axis=0)
+            for j in range(8)
+        ]
+        hidden.append(jnp.concatenate(pieces, axis=1))
     for side, (a_ref, b_ref) in enumerate(((da0_ref, db0_ref), (da1_ref, db1_ref))):
         total = 0.0
         for e, d_ref in enumerate((a_ref, b_ref)):
-            y = lax.dot_general(hidden[e], rolled(d_ref), (((1,), (1,)), ((), ())), preferred_element_type=jnp.float32)
+            y = lax.dot_general(hidden[e], d_ref[...], (((1,), (1,)), ((), ())), preferred_element_type=jnp.float32)
             total = total + weight[e] * y.astype(jnp.bfloat16).astype(jnp.float32)
         where = place_ref[0] if side == 0 else 1 - place_ref[0]
         out_ref[where] = total.astype(jnp.bfloat16)
 
 
-def down(place, parts, tail, da0, db0, da1, db1):
-    count, width = parts[0].shape[0], da0.shape[0]
+def down(place, main, rest, got, at, da0, db0, da1, db1):
+    count, width = main.shape[1] + rest.shape[1], da0.shape[0]
     vmem = pl.BlockSpec(memory_space=pltpu.VMEM)
     return pl.pallas_call(
         down_kernel,
-        in_specs=[pl.BlockSpec(memory_space=pltpu.SMEM)] + [vmem] * 13,
-        out_specs=vmem,
+        grid=(1,),
+        in_specs=[pl.BlockSpec(memory_space=pltpu.SMEM), vmem, vmem]
+        + [pl.BlockSpec((count, PAD), lambda i: (0, at // PAD))]
+        + [vmem] * 4,
+        out_specs=pl.BlockSpec((2, count, width), lambda i: (0, 0, 0)),
         out_shape=jax.ShapeDtypeStruct((2, count, width), jnp.bfloat16),
         name="down",
-    )(place, *parts, tail, da0, db0, da1, db1)
-
-
-def ring_gather(shard):
-    left = tuple((j, (j + 1) % 8) for j in range(8))
-    right = tuple((j, (j - 1) % 8) for j in range(8))
-    parts, ahead, behind = [shard], shard, shard
-    for step in range(4):
-        ahead = lax.ppermute(ahead, "zh", left)
-        parts.append(ahead)
-        if step < 3:
-            behind = lax.ppermute(behind, "zh", right)
-            parts.append(behind)
-    return parts
+    )(place, main, rest, got, da0, db0, da1, db1)
 
 
 def combine_tail(ids, comb, core, half):
@@ -143,9 +140,10 @@
     tail = combine_tail(ids, comb, core, half)
     sent = jnp.concatenate([jnp.broadcast_to(whole[None], (16, rows, depth)), tail], axis=2)
     got = lax.all_to_all(sent, XY, 0, 0, tiled=True).reshape(16 * rows, depth + PAD)
-    hidden = gate_up(place, got, wa0, wb0, wa1, wb1, depth)
-    parts = ring_gather(hidden)
-    out = down(place, parts, got[:, depth:], da0, db0, da1, db1)
+    main, rest = gate_up(place, got, wa0, wb0, wa1, wb1, depth)
+    rest = lax.all_to_all(rest, "zh", 0, 0, tiled=True)
+    main = lax.all_gather(main, "zh")
+    out = down(place, main, rest, got, depth, da0, db0, da1, db1)
     back = lax.all_to_all(out.reshape(32, rows, feats), ("zl",) + XY, 0, 0, tiled=True)
     total = jnp.sum(back.reshape(2, 16, rows, feats).astype(jnp.float32), axis=1)
     return total.reshape(2 * rows, feats).astype(jnp.bfloat16)

time: 176 us -> 182 us (1.034)
  the two profiles are of different devices: /device:TPU:1 before, /device:TPU:32 now
where the time goes in v1:
time: 182 us; the launch traced here: 181 us
  blocking collectives  58.3 us (32%)
  waiting for transfers between devices  53.7 us (30%)
  starting transfers between devices  47.8 us (26%)
  Pallas kernels  12.8 us (7%)
  other arithmetic  5.24 us (3%)
  local copies, waits for them, and re-layouts  3.35 us (2%)
    all_gather x1, blocking collectives, layer(): main = lax.all_gather(main, 'zh')  39.9 us
    ppermute x1, waiting for transfers between devices, layer(): wa1 = lax.ppermute(w_in, 'zl', swap)  19.6 us
    ppermute x1, waiting for transfers between devices, layer(): da1 = lax.ppermute(w_down, 'zl', swap)  19 us
    all_to_all x1, blocking collectives, layer(): lax.all_to_all(out.reshape(32, rows, feats), ('zl',) + XY, 0, 0, tiled=True)  18.3 us
    all_to_all x1, starting transfers between devices, layer(): lax.all_to_all(pieces.reshape(16, rows, feats), ('zh', 'zl'), 0, 0, tiled...  15.2 us
    all_to_all x1, waiting for transfers between devices, layer(): lax.all_to_all(pieces.reshape(16, rows, feats), ('zh', 'zl'), 0, 0, tiled...  15.1 us
    all_to_all x1, starting transfers between devices, layer(): rest = lax.all_to_all(rest, 'zh', 0, 0, tiled=True)  11.7 us
    pallas_call x1, Pallas kernels, gate_up(): pl.pallas_call(gate_up_kernel, grid=(depth // chunk,), in_specs=[pl.Block...  8.33 us
  transfers between devices with their start and end apart: 9, of which 3 were waited for; matrix products, arithmetic and copies ran while one was open for 3% of the time, Pallas kernels for 5%

profile of v1, /device:TPU:32, one launch (start us, length us, event | category | flops | bytes accessed | tf_op | source)
XLA Modules:
  0.0 181.3 jit_solution(4713458606908249927)
XLA Ops:
  0.0 1.5 broadcast_in_dim.30
  1.5 15.2 %all-to-all-start = ((bf16[16,16,448]{2,1,0:T(8,128)(2,1)}), bf16[16,16,448]{2,1,0:T(8,128)(2,1)S(1)}, u32[]{:S(2)}, u32[]{:S(2)}) async-start(bf16[16,16,448]{2,1,0:T(8,128)(2,1)} %bitcast.3), calls=%async_computation | async-start | bytes 524288 | tf_op jit(solution)/shard_map/all_to_all | solution.py:138
  16.7 2.0 %collective-permute-start.1 = (bf16[7168,128]{1,0:T(8,128)(2,1)}, bf16[7168,128]{1,0:T(8,128)(2,1)}, u32[]{:S(2)}, u32[]{:S(2)}) collective-permute-start(bf16[7168,128]{1,0:T(8,128)(2,1)} %bitcast.30), channel_id=1, source_target_pairs={{0,1},{1,0},{2,3},{3,2},{4,5},{5,4},{6,7},{7,6},{8,9},{9,8},{10,11... | collective-permute-start | bytes 5505032 | tf_op jit(solution)/shard_map/ppermute | solution.py:132
  18.7 0.8 slice_select_fusion.1
  19.6 0.1 copy.40
  19.6 0.8 slice_select_fusion
  20.5 0.1 copy.41
  20.5 0.1 select_reduce_fusion
  20.7 0.1 copy.42
  20.8 0.2 copy.47
  21.0 15.1 %all-to-all-done = bf16[16,16,448]{2,1,0:T(8,128)(2,1)S(1)} async-done(((bf16[16,16,448]{2,1,0:T(8,128)(2,1)}), bf16[16,16,448]{2,1,0:T(8,128)(2,1)S(1)}, u32[]{:S(2)}, u32[]{:S(2)}) %all-to-all-start) | async-done | bytes 229408 | tf_op jit(solution)/shard_map/all_to_all | solution.py:138
  36.1 0.1 copy.39
  36.3 0.3 broadcast_in_dim.31
  36.5 0.4 broadcast_in_dim.32
  36.9 2.1 %fusion.1 = bf16[16,16,7296]{2,1,0:T(8,128)(2,1)} fusion(bf16[16,16,6]{2,1,0:T(8,128)(2,1)S(1)} %copy.47, bf16[16,16,7168]{2,1,0:T(8,128)(2,1)S(1)} %broadcast_in_dim.32), kind=kLoop, calls=%fused_computation.2 | loop fusion | flops 11206656 | bytes 7408640 | tf_op jit(solution)/shard_map/concatenate | solution.py:141
  39.1 0.0 copy-start
  39.1 0.0 copy-start.1
  39.1 7.3 %all-to-all-start.1 = ((bf16[16,16,7296]{2,1,0:T(8,128)(2,1)}), bf16[16,16,7296]{2,1,0:T(8,128)(2,1)}, u32[]{:S(2)}, u32[]{:S(2)}) async-start(bf16[16,16,7296]{2,1,0:T(8,128)(2,1)} %fusion.1), calls=%async_computation.1 | async-start | bytes 7471104 | tf_op jit(solution)/shard_map/all_to_all | solution.py:142
  46.4 0.0 copy-done
  46.5 1.9 %collective-permute-start = (bf16[7168,128]{1,0:T(8,128)(2,1)S(1)}, bf16[7168,128]{1,0:T(8,128)(2,1)}, u32[]{:S(2)}, u32[]{:S(2)}) collective-permute-start(bf16[7168,128]{1,0:T(8,128)(2,1)S(1)} %bitcast.32), channel_id=1, source_target_pairs={{0,16},{16,0},{1,17},{17,1},{2,18},{18,2},{3,19},{19,3},{4,20},{20... | collective-permute-start | bytes 5505032 | tf_op jit(solution)/shard_map/ppermute | solution.py:130
  48.4 19.6 %collective-permute-done.1.wa1_ref = bf16[7168,128]{1,0:T(8,128)(2,1)} collective-permute-done((bf16[7168,128]{1,0:T(8,128)(2,1)}, bf16[7168,128]{1,0:T(8,128)(2,1)}, u32[]{:S(2)}, u32[]{:S(2)}) %collective-permute-start.1) | collective-permute-done | bytes 1835040 | tf_op jit(solution)/shard_map/ppermute | solution.py:132
  68.0 1.9 %collective-permute-start.2 = (bf16[7168,128]{1,0:T(8,128)(2,1)}, bf16[7168,128]{1,0:T(8,128)(2,1)}, u32[]{:S(2)}, u32[]{:S(2)}) collective-permute-start(bf16[7168,128]{1,0:T(8,128)(2,1)} %collective-permute-done.1.wa1_ref), channel_id=1, source_target_pairs={{0,16},{16,0},{1,17},{17,1},{2,18},{18,2},{3,19},{19,3},{4,20},{20... | collective-permute-start | bytes 5505032 | tf_op jit(solution)/shard_map/ppermute | solution.py:134
  69.9 0.0 copy-done.1
  69.9 3.7 %collective-permute-start.4 = (bf16[448,1024]{1,0:T(8,128)(2,1)S(1)}, bf16[448,1024]{1,0:T(8,128)(2,1)}, u32[]{:S(2)}, u32[]{:S(2)}) collective-permute-start(bf16[448,1024]{1,0:T(8,128)(2,1)S(1)} %bitcast.35), channel_id=1, source_target_pairs={{0,1},{1,0},{2,3},{3,2},{4,5},{5,4},{6,7},{7,6},{8,9},{9,8},{10,11... | collective-permute-start | bytes 2752520 | tf_op jit(solution)/shard_map/ppermute | solution.py:133
  73.6 2.1 %collective-permute-start.3 = (bf16[448,1024]{1,0:T(8,128)(2,1)S(1)}, bf16[448,1024]{1,0:T(8,128)(2,1)}, u32[]{:S(2)}, u32[]{:S(2)}) collective-permute-start(bf16[448,1024]{1,0:T(8,128)(2,1)S(1)} %bitcast.36), channel_id=1, source_target_pairs={{0,16},{16,0},{1,17},{17,1},{2,18},{18,2},{3,19},{19,3},{4,20},{20... | collective-permute-start | bytes 2752520 | tf_op jit(solution)/shard_map/ppermute | solution.py:131
  75.7 19.0 %collective-permute-done.4.da1_ref = bf16[448,1024]{1,0:T(8,128)(2,1)} collective-permute-done((bf16[448,1024]{1,0:T(8,128)(2,1)S(1)}, bf16[448,1024]{1,0:T(8,128)(2,1)}, u32[]{:S(2)}, u32[]{:S(2)}) %collective-permute-start.4) | collective-permute-done | bytes 917536 | tf_op jit(solution)/shard_map/ppermute | solution.py:133
  94.7 1.9 %collective-permute-start.5 = (bf16[448,1024]{1,0:T(8,128)(2,1)}, bf16[448,1024]{1,0:T(8,128)(2,1)}, u32[]{:S(2)}, u32[]{:S(2)}) collective-permute-start(bf16[448,1024]{1,0:T(8,128)(2,1)} %collective-permute-done.4.da1_ref), channel_id=1, source_target_pairs={{0,16},{16,0},{1,17},{17,1},{2,18},{18,2},{3,19},{19,3},{4,20},{20... | collective-permute-start | bytes 2752520 | tf_op jit(solution)/shard_map/ppermute | solution.py:135
  96.6 0.6 pad_add_fusion.half_ref.place_ref
  97.2 0.0 collective-permute-done.wb0_ref
  97.2 0.0 collective-permute-done.2.wb1_ref
  97.2 0.0 all-to-all-done.1
  97.2 8.3 %gate_up.1 = (bf16[240,256]{1,0:T(8,128)(2,1)}, bf16[8,16,256]{2,1,0:T(8,128)(2,1)}) custom-call(s32[2]{0:T(128)} %pad_add_fusion.half_ref.place_ref, bf16[256,7296]{1,0:T(8,128)(2,1)} %bitcast.12.rows_ref.tail_ref, bf16[7168,128]{1,0:T(8,128)(2,1)} %bitcast.31, bf16[7168,128]{1,0:T(8,128)(2,1)} %collective-permute-done.wb0_ref, ...), custom_call_target="tpu_custom_call" | custom-call | tf_op jit(solution)/shard_map/gate_up/pallas_call | solution.py:48
  105.6 11.7 %all-to-all-start.2 = ((bf16[8,16,256]{2,1,0:T(8,128)(2,1)}), bf16[8,16,256]{2,1,0:T(8,128)(2,1)S(1)}, u32[]{:S(2)}, u32[]{:S(2)}) async-start(bf16[8,16,256]{2,1,0:T(8,128)(2,1)} %get-tuple-element.8), calls=%async_computation.2 | async-start | bytes 131072 | tf_op jit(solution)/shard_map/all_to_all | solution.py:144
  117.3 39.9 %all-gather = bf16[1920,256]{1,0:T(8,128)(2,1)} all-gather(bf16[240,256]{1,0:T(8,128)(2,1)} %get-tuple-element.7), channel_id=2, replica_groups=mesh['x'=4,'y'=4,'c'=2,'zh'=8,'zl'=2] {'zh'}, dimensions={0}, use_global_device_ids=true | all-gather | bytes 1105920 | tf_op jit(solution)/shard_map/all_gather | solution.py:145
  157.2 0.0 collective-permute-done.3.db0_ref
  157.2 0.0 collective-permute-done.5.db1_ref
  157.2 0.0 all-to-all-done.2.rest_ref
  157.2 0.0 copy-start.2
  157.2 0.6 copy-done.2
  157.8 4.4 %down.1 = bf16[2,256,448]{2,1,0:T(8,128)(2,1)} custom-call(s32[2]{0:T(128)} %pad_add_fusion.half_ref.place_ref, bf16[8,240,256]{2,1,0:T(8,128)(2,1)} %bitcast.28, bf16[8,16,256]{2,1,0:T(8,128)(2,1)} %copy-done.2, bf16[256,7296]{1,0:T(8,128)(2,1)} %bitcast.12.rows_ref.tail_ref, bf16[448,1024]{1,0:T(8,128)(2,1)} %bitcast.34, ...), custom_call_target="tpu_custom_call" | custom-call | tf_op jit(solution)/shard_map/down/pallas_call | solution.py:94
  162.3 18.3 %all_to_all.20 = bf16[32,16,448]{2,1,0:T(8,128)(2,1)S(1)} all-to-all(bf16[32,16,448]{2,1,0:T(8,128)(2,1)} %bitcast.29), channel_id=1, replica_groups=mesh['x'=4,'y'=4,'c'=2,'zh'=8,'zl'=2] {'zl','x','y'}, dimensions={0} | all-to-all | bytes 917504 | tf_op jit(solution)/shard_map/all_to_all | solution.py:147
  180.6 0.7 bitcast_reduce_fusion
  (4 shorter events, 0.0 us)
Async XLA Ops:
  1.5 34.6 %all-to-all-start = ((bf16[16,16,448]{2,1,0:T(8,128)(2,1)}), bf16[16,16,448]{2,1,0:T(8,128)(2,1)S(1)}, u32[]{:S(2)}, u32[]{:S(2)}) async-start(bf16[16,16,448]{2,1,0:T(8,128)(2,1)} %bitcast.3), calls=%async_computation | async-start | bytes 524288 | tf_op jit(solution)/shard_map/all_to_all | solution.py:138
  16.7 51.3 %collective-permute-start.1 = (bf16[7168,128]{1,0:T(8,128)(2,1)}, bf16[7168,128]{1,0:T(8,128)(2,1)}, u32[]{:S(2)}, u32[]{:S(2)}) collective-permute-start(bf16[7168,128]{1,0:T(8,128)(2,1)} %bitcast.30), channel_id=1, source_target_pairs={{0,1},{1,0},{2,3},{3,2},{4,5},{5,4},{6,7},{7,6},{8,9},{9,8},{10,11... | collective-permute-start | bytes 5505032 | tf_op jit(solution)/shard_map/ppermute | solution.py:132
  39.1 7.4 %copy-start = (bf16[1,7168,128]{2,1,0:T(8,128)(2,1)S(1)}, bf16[1,7168,128]{2,1,0:T(8,128)(2,1)}, u32[]{:S(2)}) copy-start(bf16[1,7168,128]{2,1,0:T(8,128)(2,1)} %param.8) | copy-start | bytes 5505028
  39.1 30.8 %copy-start.1 = (bf16[1,1024,448]{1,2,0:T(8,128)(2,1)S(1)}, bf16[1,1024,448]{1,2,0:T(8,128)(2,1)}, u32[]{:S(2)}) copy-start(bf16[1,1024,448]{1,2,0:T(8,128)(2,1)} %param.9) | copy-start | bytes 2752516
  39.1 58.1 %all-to-all-start.1 = ((bf16[16,16,7296]{2,1,0:T(8,128)(2,1)}), bf16[16,16,7296]{2,1,0:T(8,128)(2,1)}, u32[]{:S(2)}, u32[]{:S(2)}) async-start(bf16[16,16,7296]{2,1,0:T(8,128)(2,1)} %fusion.1), calls=%async_computation.1 | async-start | bytes 7471104 | tf_op jit(solution)/shard_map/all_to_all | solution.py:142
  46.5 50.8 %collective-permute-start = (bf16[7168,128]{1,0:T(8,128)(2,1)S(1)}, bf16[7168,128]{1,0:T(8,128)(2,1)}, u32[]{:S(2)}, u32[]{:S(2)}) collective-permute-start(bf16[7168,128]{1,0:T(8,128)(2,1)S(1)} %bitcast.32), channel_id=1, source_target_pairs={{0,16},{16,0},{1,17},{17,1},{2,18},{18,2},{3,19},{19,3},{4,20},{20... | collective-permute-start | bytes 5505032 | tf_op jit(solution)/shard_map/ppermute | solution.py:130
  68.0 29.3 %collective-permute-start.2 = (bf16[7168,128]{1,0:T(8,128)(2,1)}, bf16[7168,128]{1,0:T(8,128)(2,1)}, u32[]{:S(2)}, u32[]{:S(2)}) collective-permute-start(bf16[7168,128]{1,0:T(8,128)(2,1)} %collective-permute-done.1.wa1_ref), channel_id=1, source_target_pairs={{0,16},{16,0},{1,17},{17,1},{2,18},{18,2},{3,19},{19,3},{4,20},{20... | collective-permute-start | bytes 5505032 | tf_op jit(solution)/shard_map/ppermute | solution.py:134
  69.9 24.8 %collective-permute-start.4 = (bf16[448,1024]{1,0:T(8,128)(2,1)S(1)}, bf16[448,1024]{1,0:T(8,128)(2,1)}, u32[]{:S(2)}, u32[]{:S(2)}) collective-permute-start(bf16[448,1024]{1,0:T(8,128)(2,1)S(1)} %bitcast.35), channel_id=1, source_target_pairs={{0,1},{1,0},{2,3},{3,2},{4,5},{5,4},{6,7},{7,6},{8,9},{9,8},{10,11... | collective-permute-start | bytes 2752520 | tf_op jit(solution)/shard_map/ppermute | solution.py:133
  73.6 83.6 %collective-permute-start.3 = (bf16[448,1024]{1,0:T(8,128)(2,1)S(1)}, bf16[448,1024]{1,0:T(8,128)(2,1)}, u32[]{:S(2)}, u32[]{:S(2)}) collective-permute-start(bf16[448,1024]{1,0:T(8,128)(2,1)S(1)} %bitcast.36), channel_id=1, source_target_pairs={{0,16},{16,0},{1,17},{17,1},{2,18},{18,2},{3,19},{19,3},{4,20},{20... | collective-permute-start | bytes 2752520 | tf_op jit(solution)/shard_map/ppermute | solution.py:131
  94.7 62.5 %collective-permute-start.5 = (bf16[448,1024]{1,0:T(8,128)(2,1)}, bf16[448,1024]{1,0:T(8,128)(2,1)}, u32[]{:S(2)}, u32[]{:S(2)}) collective-permute-start(bf16[448,1024]{1,0:T(8,128)(2,1)} %collective-permute-done.4.da1_ref), channel_id=1, source_target_pairs={{0,16},{16,0},{1,17},{17,1},{2,18},{18,2},{3,19},{19,3},{4,20},{20... | collective-permute-start | bytes 2752520 | tf_op jit(solution)/shard_map/ppermute | solution.py:135
  105.6 51.6 %all-to-all-start.2 = ((bf16[8,16,256]{2,1,0:T(8,128)(2,1)}), bf16[8,16,256]{2,1,0:T(8,128)(2,1)S(1)}, u32[]{:S(2)}, u32[]{:S(2)}) async-start(bf16[8,16,256]{2,1,0:T(8,128)(2,1)} %get-tuple-element.8), calls=%async_computation.2 | async-start | bytes 131072 | tf_op jit(solution)/shard_map/all_to_all | solution.py:144
  157.2 0.6 copy-start.2

commit v2 on v0

v2 whole, which is shorter than its diff:
```python
import jax
import jax.numpy as jnp
from jax import lax
from jax.experimental import pallas as pl
from jax.experimental.pallas import tpu as pltpu
from jax.sharding import Mesh, PartitionSpec as P


XY = ("x", "y")
PAD = 128
HOPS = (0, 7, 1, 6, 2, 5, 3, 4)


def gate_up_kernel(half_ref, rows_ref, wa0_ref, wa1_ref, wb0_ref, wb1_ref, out_ref, rows_buf, w_buf, acc_ref, sems):
    depth = wa0_ref.shape[0]
    chunks = sems.shape[0]
    chunk = depth // chunks

    def copies(k):
        span = pl.ds(k * chunk, chunk)
        yield pltpu.make_async_copy(rows_ref.at[:, span], rows_buf.at[:, span], sems.at[k, 0])
        for i, w_ref in enumerate((wa0_ref, wa1_ref, wb0_ref, wb1_ref)):
            yield pltpu.make_async_copy(w_ref.at[span, :], w_buf.at[span, pl.ds(128 * i, 128)], sems.at[k, i + 1])

    for k in range(chunks):
        for copy in copies(k):
            copy.start()
    for k in range(chunks):
        for copy in copies(k):
            copy.wait()
        span = pl.ds(k * chunk, chunk)
        part = jnp.dot(rows_buf[:, span], w_buf[span, :], preferred_element_type=jnp.float32)
        acc_ref[...] = part if k == 0 else acc_ref[...] + part

    lane = lax.broadcasted_iota(jnp.int32, (rows_ref.shape[0], 128), 1)
    low = lane < 64
    first = jnp.where(low, 0, 1) == half_ref[0]

    def hidden(at):
        value = acc_ref[:, at : at + 128]
        turned = pltpu.roll(value, 64, 1)
        gate = jnp.where(low, value, turned)
        up = jnp.where(low, turned, value)
        return gate / (1.0 + jnp.exp(-gate)) * up

    for e in range(2):
        both = jnp.where(first, hidden(256 * e), hidden(256 * e + 128))
        out_ref[:, 128 * e : 128 * e + 128] = both.astype(jnp.bfloat16)


def gate_up(half, rows, wa0, wa1, wb0, wb1):
    count, depth = rows.shape[0], wa0.shape[0]
    return pl.pallas_call(
        gate_up_kernel,
        in_specs=[pl.BlockSpec(memory_space=pltpu.SMEM)] + [pl.BlockSpec(memory_space=pl.ANY)] * 5,
        out_specs=pl.BlockSpec(memory_space=pltpu.VMEM),
        out_shape=jax.ShapeDtypeStruct((count, 256), jnp.bfloat16),
        scratch_shapes=[
            pltpu.VMEM((count, depth), jnp.bfloat16),
            pltpu.VMEM((depth, 512), jnp.bfloat16),
            pltpu.VMEM((count, 512), jnp.float32),
            pltpu.SemaphoreType.DMA((7, 5)),
        ],
        name="gate_up",
    )(half, rows, wa0, wa1, wb0, wb1)


def down_kernel(place_ref, h0_ref, h1, h2, h3, h4, h5, h6, h7, rows_ref, da0_ref, db0_ref, da1_ref, db1_ref, out_ref, d_buf, h_buf, tail_buf, sems):
    copies = [pltpu.make_async_copy(ref, d_buf.at[i], sems.at[i]) for i, ref in enumerate((da0_ref, db0_ref, da1_ref))]
    own_copy = pltpu.make_async_copy(h0_ref, h_buf, sems.at[3])
    tail_copy = pltpu.make_async_copy(rows_ref.at[:, pl.ds(rows_ref.shape[1] - PAD, PAD)], tail_buf, sems.at[4])
    for copy in (own_copy, tail_copy, *copies):
        copy.start()
    own_copy.wait()
    parts = (h_buf, h1, h2, h3, h4, h5, h6, h7)
    hidden = [jnp.concatenate([part[:, 128 * e : 128 * e + 128] for part in parts], axis=1) for e in range(2)]
    starts = [pl.multiple_of(lax.rem(place_ref[1] + by, 8) * 128, 128) for by in HOPS]
    tail_copy.wait()
    tail = tail_buf[...].astype(jnp.float32)
    weight = [
        tail[:, 3 * e : 3 * e + 1] + tail[:, 3 * e + 1 : 3 * e + 2] + tail[:, 3 * e + 2 : 3 * e + 3] for e in range(2)
    ]
    for side in range(2):
        total = 0.0
        for e in range(2):
            i = 2 * side + e
            if i < 3:
                copies[i].wait()
            d_ref = d_buf.at[i] if i < 3 else db1_ref
            rolled = jnp.concatenate([d_ref[:, pl.ds(start, 128)] for start in starts], axis=1)
            y = lax.dot_general(hidden[e], rolled, (((1,), (1,)), ((), ())), preferred_element_type=jnp.float32)
            total = total + weight[e] * y.astype(jnp.bfloat16).astype(jnp.float32)
        where = place_ref[0] if side == 0 else 1 - place_ref[0]
        out_ref[where] = total.astype(jnp.bfloat16)


def down(place, parts, rows, da0, db0, da1, db1):
    count, width = parts[0].shape[0], da0.shape[0]
    vmem, anywhere = pl.BlockSpec(memory_space=pltpu.VMEM), pl.BlockSpec(memory_space=pl.ANY)
    *parts, db1 = [parts[0]] + [pltpu.with_memory_space_constraint(a, pltpu.VMEM) for a in (*parts[1:], db1)]
    return pl.pallas_call(
        down_kernel,
        in_specs=[pl.BlockSpec(memory_space=pltpu.SMEM)] + [anywhere] + [vmem] * 7 + [anywhere] * 4 + [vmem],
        out_specs=vmem,
        out_shape=jax.ShapeDtypeStruct((2, count, width), jnp.bfloat16),
        scratch_shapes=[
            pltpu.VMEM((3, width, da0.shape[1]), jnp.bfloat16),
            pltpu.VMEM((count, 256), jnp.bfloat16),
            pltpu.VMEM((count, PAD), jnp.bfloat16),
            pltpu.SemaphoreType.DMA((5,)),
        ],
        name="down",
    )(place, *parts, rows, da0, db0, da1, db1)


def ring_gather(shard):
    left = tuple((j, (j + 1) % 8) for j in range(8))
    right = tuple((j, (j - 1) % 8) for j in range(8))
    parts, ahead, behind = [shard], shard, shard
    for step in range(4):
        ahead = lax.ppermute(ahead, "zh", left)
        parts.append(ahead)
        if step < 3:
            behind = lax.ppermute(behind, "zh", right)
            parts.append(behind)
    return parts


def combine_tail(ids, comb, core, half):
    rows, experts = ids.shape[0] // 2, 32
    ids = jnp.where(half == 0, ids[:rows], ids[rows:])
    comb = jnp.where(half == 0, comb[:rows], comb[rows:])
    hit = ids[:, :, None] == jnp.arange(experts, dtype=jnp.int32)[None, None, :]
    dense = jnp.sum(jnp.where(hit, comb[:, :, None], 0.0), axis=1)
    dense = jnp.transpose(dense.reshape(rows, experts // 2, 2), (1, 0, 2))
    pair = jnp.where(core == 0, dense, dense[:, :, ::-1])
    high = lax.reduce_precision(pair, 8, 7)
    middle = lax.reduce_precision(pair - high, 8, 7)
    low = lax.reduce_precision(pair - high - middle, 8, 7)
    pieces = jnp.stack([high, middle, low], axis=3).reshape(experts // 2, rows, 6)
    return jnp.pad(pieces.astype(jnp.bfloat16), ((0, 0), (0, 0), (0, PAD - 6)))


def layer(tokens, ids, comb, w_in, w_down):
    core, half = lax.axis_index("c"), lax.axis_index("zl")
    place = jnp.stack([half, lax.axis_index("zh")]).astype(jnp.int32)
    swap = ((0, 1), (1, 0))
    w_in, w_down = w_in[0], w_down[0].T
    rows, feats = tokens.shape[0] // 2, tokens.shape[1]
    depth = w_in.shape[0]

    wa0, da0 = w_in, w_down
    wb0 = lax.ppermute(w_in, "c", swap)
    db0 = lax.ppermute(w_down, "c", swap)
    wa1 = lax.ppermute(w_in, "zl", swap)
    da1 = lax.ppermute(w_down, "zl", swap)
    wb1 = lax.ppermute(wa1, "c", swap)
    db1 = lax.ppermute(da1, "c", swap)

    pieces = jnp.broadcast_to(tokens.reshape(1, 2, rows, feats), (8, 2, rows, feats))
    pieces = lax.all_to_all(pieces.reshape(16, rows, feats), ("zh", "zl"), 0, 0, tiled=True)
    whole = jnp.transpose(pieces, (1, 0, 2)).reshape(rows, depth)
    tail = combine_tail(ids, comb, core, half)
    sent = jnp.concatenate([jnp.broadcast_to(whole[None], (16, rows, depth)), tail], axis=2)
    got = lax.all_to_all(sent, XY, 0, 0, tiled=True).reshape(16 * rows, depth + PAD)
    hidden = gate_up(place, got, wa0, wa1, wb0, wb1)
    parts = ring_gather(hidden)
    out = down(place, parts, got, da0, db0, da1, db1)
    back = lax.all_to_all(out.reshape(32, rows, feats), ("zl",) + XY, 0, 0, tiled=True)
    total = jnp.sum(back.reshape(2, 16, rows, feats).astype(jnp.float32), axis=1)
    return total.reshape(2 * rows, feats).astype(jnp.bfloat16)


def solution(mesh):
    fine = Mesh(mesh.devices.reshape(4, 4, 2, 8, 2), ("x", "y", "c", "zh", "zl"))
    e, t = ("x", "y", "c"), ("zh", "zl")
    in_specs = (P(e, t), P(e, None), P(e, None), P(e, None, t), P(e, None, t))
    return jax.shard_map(layer, mesh=fine, in_specs=in_specs, out_specs=P(e, t), check_vma=False)
```

time: 176 us -> 173 us (0.983)
  local copies, waits for them, and re-layouts: 4.87 us -> 2.73 us
  Pallas kernels: 12.9 us -> 10.9 us
  waiting for transfers between devices: 65.1 us -> 66.9 us
    pallas_call x1, Pallas kernels: 8.27 us -> 6.36 us  [gate_up(): pl.pallas_call(gate_up_kernel, in_specs=[pl.BlockSpec(memory_space=pltpu....]
  transfers between devices with their start and end apart: 15 -> 15, of which waited for: 8 -> 8; matrix products, arithmetic and copies ran while one was open for 4% -> 3% of each run, Pallas kernels for 5% -> 4%
where the time goes in v2:
time: 173 us; the launch traced here: 172 us
  starting transfers between devices  69.4 us (40%)
  waiting for transfers between devices  66.9 us (39%)
  blocking collectives  16.6 us (10%)
  Pallas kernels  10.9 us (6%)
  other arithmetic  5.26 us (3%)
  local copies, waits for them, and re-layouts  2.73 us (2%)
    ppermute x1, waiting for transfers between devices, layer(): wa1 = lax.ppermute(w_in, 'zl', swap)  21 us
    ppermute x1, waiting for transfers between devices, layer(): da1 = lax.ppermute(w_down, 'zl', swap)  20 us
    all_to_all x1, blocking collectives, layer(): lax.all_to_all(out.reshape(32, rows, feats), ('zl',) + XY, 0, 0, tiled=True)  16.6 us
    all_to_all x1, starting transfers between devices, layer(): lax.all_to_all(pieces.reshape(16, rows, feats), ('zh', 'zl'), 0, 0, tiled...  15.7 us
    ppermute x4, starting transfers between devices, ring_gather(): ahead = lax.ppermute(ahead, 'zh', left)  15.2 us
    ppermute x3, starting transfers between devices, ring_gather(): behind = lax.ppermute(behind, 'zh', right)  10.3 us
    ppermute x3, waiting for transfers between devices, ring_gather(): behind = lax.ppermute(behind, 'zh', right)  10.1 us
    all_to_all x1, waiting for transfers between devices, layer(): lax.all_to_all(pieces.reshape(16, rows, feats), ('zh', 'zl'), 0, 0, tiled...  8.24 us
  transfers between devices with their start and end apart: 15, of which 8 were waited for; matrix products, arithmetic and copies ran while one was open for 3% of the time, Pallas kernels for 4%

profile of v2, /device:TPU:1, one launch (start us, length us, event | category | flops | bytes accessed | tf_op | source)
XLA Modules:
  0.0 171.9 jit_solution(121923168470503681)
XLA Ops:
  0.0 1.5 broadcast_in_dim.30
  1.5 15.7 %all-to-all-start = ((bf16[16,16,448]{2,1,0:T(8,128)(2,1)}), bf16[16,16,448]{2,1,0:T(8,128)(2,1)S(1)}, u32[]{:S(2)}, u32[]{:S(2)}) async-start(bf16[16,16,448]{2,1,0:T(8,128)(2,1)} %bitcast.3), calls=%async_computation | async-start | bytes 524288 | tf_op jit(solution)/shard_map/all_to_all | solution.py:161
  17.2 3.3 %collective-permute-start = (bf16[7168,128]{1,0:T(8,128)(2,1)}, bf16[7168,128]{1,0:T(8,128)(2,1)}, u32[]{:S(2)}, u32[]{:S(2)}) collective-permute-start(bf16[7168,128]{1,0:T(8,128)(2,1)} %bitcast.28), channel_id=1, source_target_pairs={{0,1},{1,0},{2,3},{3,2},{4,5},{5,4},{6,7},{7,6},{8,9},{9,8},{10,11... | collective-permute-start | bytes 5505032 | tf_op jit(solution)/shard_map/ppermute | solution.py:155
  20.5 0.8 slice_select_fusion.1
  21.3 0.1 copy.40
  21.4 0.8 slice_select_fusion
  22.2 0.1 copy.41
  22.3 0.1 select_reduce_fusion
  22.4 0.1 copy.42
  22.6 0.2 copy.47
  22.8 8.2 %all-to-all-done = bf16[16,16,448]{2,1,0:T(8,128)(2,1)S(1)} async-done(((bf16[16,16,448]{2,1,0:T(8,128)(2,1)}), bf16[16,16,448]{2,1,0:T(8,128)(2,1)S(1)}, u32[]{:S(2)}, u32[]{:S(2)}) %all-to-all-start) | async-done | bytes 229408 | tf_op jit(solution)/shard_map/all_to_all | solution.py:161
  31.0 0.1 copy.39
  31.1 0.3 broadcast_in_dim.31
  31.4 0.4 broadcast_in_dim.32
  31.8 2.2 %fusion.1 = bf16[16,16,7296]{2,1,0:T(8,128)(2,1)} fusion(bf16[16,16,6]{2,1,0:T(8,128)(2,1)S(1)} %copy.47, bf16[16,16,7168]{2,1,0:T(8,128)(2,1)S(1)} %broadcast_in_dim.32), kind=kLoop, calls=%fused_computation.2 | loop fusion | flops 11206656 | bytes 7408640 | tf_op jit(solution)/shard_map/concatenate | solution.py:164
  34.0 0.0 copy-start
  34.0 6.9 %all-to-all-start.1 = ((bf16[16,16,7296]{2,1,0:T(8,128)(2,1)}), bf16[16,16,7296]{2,1,0:T(8,128)(2,1)}, u32[]{:S(2)}, u32[]{:S(2)}) async-start(bf16[16,16,7296]{2,1,0:T(8,128)(2,1)} %fusion.1), calls=%async_computation.1 | async-start | bytes 7471104 | tf_op jit(solution)/shard_map/all_to_all | solution.py:165
  40.9 0.0 copy-done
  40.9 7.8 %collective-permute-start.1 = (bf16[7168,128]{1,0:T(8,128)(2,1)S(1)}, bf16[7168,128]{1,0:T(8,128)(2,1)}, u32[]{:S(2)}, u32[]{:S(2)}) collective-permute-start(bf16[7168,128]{1,0:T(8,128)(2,1)S(1)} %bitcast.30), channel_id=1, source_target_pairs={{0,16},{16,0},{1,17},{17,1},{2,18},{18,2},{3,19},{19,3},{4,20},{20... | collective-permute-start | bytes 5505032 | tf_op jit(solution)/shard_map/ppermute | solution.py:153
  48.7 21.0 %collective-permute-done.wa1_ref = bf16[7168,128]{1,0:T(8,128)(2,1)} collective-permute-done((bf16[7168,128]{1,0:T(8,128)(2,1)}, bf16[7168,128]{1,0:T(8,128)(2,1)}, u32[]{:S(2)}, u32[]{:S(2)}) %collective-permute-start) | collective-permute-done | bytes 1835040 | tf_op jit(solution)/shard_map/ppermute | solution.py:155
  69.7 3.3 %collective-permute-start.2 = (bf16[7168,128]{1,0:T(8,128)(2,1)}, bf16[7168,128]{1,0:T(8,128)(2,1)}, u32[]{:S(2)}, u32[]{:S(2)}) collective-permute-start(bf16[7168,128]{1,0:T(8,128)(2,1)} %collective-permute-done.wa1_ref), channel_id=1, source_target_pairs={{0,16},{16,0},{1,17},{17,1},{2,18},{18,2},{3,19},{19,3},{4,20},{20... | collective-permute-start | bytes 5505032 | tf_op jit(solution)/shard_map/ppermute | solution.py:157
  73.0 1.9 %collective-permute-start.11 = (bf16[448,1024]{1,0:T(8,128)(2,1)}, bf16[448,1024]{1,0:T(8,128)(2,1)}, u32[]{:S(2)}, u32[]{:S(2)}) collective-permute-start(bf16[448,1024]{1,0:T(8,128)(2,1)} %bitcast.15.da0_ref), channel_id=1, source_target_pairs={{0,1},{1,0},{2,3},{3,2},{4,5},{5,4},{6,7},{7,6},{8,9},{9,8},{10,11... | collective-permute-start | bytes 2752520 | tf_op jit(solution)/shard_map/ppermute | solution.py:156
  75.0 2.2 %collective-permute-start.10 = (bf16[448,1024]{1,0:T(8,128)(2,1)}, bf16[448,1024]{1,0:T(8,128)(2,1)}, u32[]{:S(2)}, u32[]{:S(2)}) collective-permute-start(bf16[448,1024]{1,0:T(8,128)(2,1)} %bitcast.15.da0_ref), channel_id=1, source_target_pairs={{0,16},{16,0},{1,17},{17,1},{2,18},{18,2},{3,19},{19,3},{4,20},{20... | collective-permute-start | bytes 2752520 | tf_op jit(solution)/shard_map/ppermute | solution.py:154
  77.1 20.0 %collective-permute-done.11.da1_ref = bf16[448,1024]{1,0:T(8,128)(2,1)} collective-permute-done((bf16[448,1024]{1,0:T(8,128)(2,1)}, bf16[448,1024]{1,0:T(8,128)(2,1)}, u32[]{:S(2)}, u32[]{:S(2)}) %collective-permute-start.11) | collective-permute-done | bytes 917536 | tf_op jit(solution)/shard_map/ppermute | solution.py:156
  97.2 2.8 %collective-permute-start.12 = (bf16[448,1024]{1,0:T(8,128)(2,1)}, bf16[448,1024]{1,0:T(8,128)(2,1)S(1)}, u32[]{:S(2)}, u32[]{:S(2)}) collective-permute-start(bf16[448,1024]{1,0:T(8,128)(2,1)} %collective-permute-done.11.da1_ref), channel_id=1, source_target_pairs={{0,16},{16,0},{1,17},{17,1},{2,18},{18,2},{3,19},{19,3},{4,20},{20... | collective-permute-start | bytes 2752520 | tf_op jit(solution)/shard_map/ppermute | solution.py:158
  99.9 0.6 pad_add_fusion.half_ref.place_ref
  100.5 0.0 collective-permute-done.1.wb0_ref
  100.5 0.0 collective-permute-done.2.wb1_ref
  100.5 0.0 all-to-all-done.1
  100.6 6.4 %gate_up.1.h0_ref = bf16[256,256]{1,0:T(8,128)(2,1)} custom-call(s32[2]{0:T(128)} %pad_add_fusion.half_ref.place_ref, bf16[256,7296]{1,0:T(8,128)(2,1)} %bitcast.12.rows_ref, bf16[7168,128]{1,0:T(8,128)(2,1)} %bitcast.29, bf16[7168,128]{1,0:T(8,128)(2,1)} %collective-permute-done.wa1_ref, bf16[7168,128]{1,0:T(8,128)(2,1)} %collective-permute-done.1.wb0_ref, ...), custom_call_target="tpu_custom_call" | custom-call | tf_op jit(solution)/shard_map/gate_up/pallas_call | solution.py:53
  106.9 4.1 %collective-permute-start.3 = (bf16[256,256]{1,0:T(8,128)(2,1)}, bf16[256,256]{1,0:T(8,128)(2,1)S(1)}, u32[]{:S(2)}, u32[]{:S(2)}) collective-permute-start(bf16[256,256]{1,0:T(8,128)(2,1)} %gate_up.1.h0_ref), channel_id=1, source_target_pairs={{0,2},{2,4},{4,6},{6,8},{8,10},{10,12},{12,14},{14,0},{1,3},{3,5},... | collective-permute-start | bytes 393224 | tf_op jit(solution)/shard_map/ppermute | solution.py:121
  111.0 3.3 %collective-permute-start.4 = (bf16[256,256]{1,0:T(8,128)(2,1)}, bf16[256,256]{1,0:T(8,128)(2,1)S(1)}, u32[]{:S(2)}, u32[]{:S(2)}) collective-permute-start(bf16[256,256]{1,0:T(8,128)(2,1)} %gate_up.1.h0_ref), channel_id=1, source_target_pairs={{0,14},{2,0},{4,2},{6,4},{8,6},{10,8},{12,10},{14,12},{1,15},{3,1}... | collective-permute-start | bytes 393224 | tf_op jit(solution)/shard_map/ppermute | solution.py:124
  114.3 2.0 %collective-permute-done.3.h1 = bf16[256,256]{1,0:T(8,128)(2,1)S(1)} collective-permute-done((bf16[256,256]{1,0:T(8,128)(2,1)}, bf16[256,256]{1,0:T(8,128)(2,1)S(1)}, u32[]{:S(2)}, u32[]{:S(2)}) %collective-permute-start.3) | collective-permute-done | bytes 131104 | tf_op jit(solution)/shard_map/ppermute | solution.py:121
  116.3 4.5 %collective-permute-start.5 = (bf16[256,256]{1,0:T(8,128)(2,1)S(1)}, bf16[256,256]{1,0:T(8,128)(2,1)S(1)}, u32[]{:S(2)}, u32[]{:S(2)}) collective-permute-start(bf16[256,256]{1,0:T(8,128)(2,1)S(1)} %collective-permute-done.3.h1), channel_id=1, source_target_pairs={{0,2},{2,4},{4,6},{6,8},{8,10},{10,12},{12,14},{14,0},{1,3},{3,5},... | collective-permute-start | bytes 393224 | tf_op jit(solution)/shard_map/ppermute | solution.py:121
  120.8 2.2 %collective-permute-done.4.h2 = bf16[256,256]{1,0:T(8,128)(2,1)S(1)} collective-permute-done((bf16[256,256]{1,0:T(8,128)(2,1)}, bf16[256,256]{1,0:T(8,128)(2,1)S(1)}, u32[]{:S(2)}, u32[]{:S(2)}) %collective-permute-start.4) | collective-permute-done | bytes 131104 | tf_op jit(solution)/shard_map/ppermute | solution.py:124
  123.0 3.5 %collective-permute-start.6 = (bf16[256,256]{1,0:T(8,128)(2,1)S(1)}, bf16[256,256]{1,0:T(8,128)(2,1)S(1)}, u32[]{:S(2)}, u32[]{:S(2)}) collective-permute-start(bf16[256,256]{1,0:T(8,128)(2,1)S(1)} %collective-permute-done.4.h2), channel_id=1, source_target_pairs={{0,14},{2,0},{4,2},{6,4},{8,6},{10,8},{12,10},{14,12},{1,15},{3,1}... | collective-permute-start | bytes 393224 | tf_op jit(solution)/shard_map/ppermute | solution.py:124
  126.5 0.0 collective-permute-done.5.h3
  126.5 3.8 %collective-permute-start.7 = (bf16[256,256]{1,0:T(8,128)(2,1)S(1)}, bf16[256,256]{1,0:T(8,128)(2,1)S(1)}, u32[]{:S(2)}, u32[]{:S(2)}) collective-permute-start(bf16[256,256]{1,0:T(8,128)(2,1)S(1)} %collective-permute-done.5.h3), channel_id=1, source_target_pairs={{0,2},{2,4},{4,6},{6,8},{8,10},{10,12},{12,14},{14,0},{1,3},{3,5},... | collective-permute-start | bytes 393224 | tf_op jit(solution)/shard_map/ppermute | solution.py:121
  130.4 4.5 %collective-permute-done.6.h4 = bf16[256,256]{1,0:T(8,128)(2,1)S(1)} collective-permute-done((bf16[256,256]{1,0:T(8,128)(2,1)S(1)}, bf16[256,256]{1,0:T(8,128)(2,1)S(1)}, u32[]{:S(2)}, u32[]{:S(2)}) %collective-permute-start.6) | collective-permute-done | bytes 131104 | tf_op jit(solution)/shard_map/ppermute | solution.py:124
  134.8 3.5 %collective-permute-start.8 = (bf16[256,256]{1,0:T(8,128)(2,1)S(1)}, bf16[256,256]{1,0:T(8,128)(2,1)S(1)}, u32[]{:S(2)}, u32[]{:S(2)}) collective-permute-start(bf16[256,256]{1,0:T(8,128)(2,1)S(1)} %collective-permute-done.6.h4), channel_id=1, source_target_pairs={{0,14},{2,0},{4,2},{6,4},{8,6},{10,8},{12,10},{14,12},{1,15},{3,1}... | collective-permute-start | bytes 393224 | tf_op jit(solution)/shard_map/ppermute | solution.py:124
  138.4 0.0 collective-permute-done.7.h5
  138.4 2.8 %collective-permute-start.9 = (bf16[256,256]{1,0:T(8,128)(2,1)S(1)}, bf16[256,256]{1,0:T(8,128)(2,1)S(1)}, u32[]{:S(2)}, u32[]{:S(2)}) collective-permute-start(bf16[256,256]{1,0:T(8,128)(2,1)S(1)} %collective-permute-done.7.h5), channel_id=1, source_target_pairs={{0,2},{2,4},{4,6},{6,8},{8,10},{10,12},{12,14},{14,0},{1,3},{3,5},... | collective-permute-start | bytes 393224 | tf_op jit(solution)/shard_map/ppermute | solution.py:121
  141.2 0.0 collective-permute-done.10.db0_ref
  141.2 0.0 collective-permute-done.12.db1_ref
  141.2 3.4 %collective-permute-done.8.h6 = bf16[256,256]{1,0:T(8,128)(2,1)S(1)} collective-permute-done((bf16[256,256]{1,0:T(8,128)(2,1)S(1)}, bf16[256,256]{1,0:T(8,128)(2,1)S(1)}, u32[]{:S(2)}, u32[]{:S(2)}) %collective-permute-start.8) | collective-permute-done | bytes 131104 | tf_op jit(solution)/shard_map/ppermute | solution.py:124
  144.6 5.5 %collective-permute-done.9.h7 = bf16[256,256]{1,0:T(8,128)(2,1)S(1)} collective-permute-done((bf16[256,256]{1,0:T(8,128)(2,1)S(1)}, bf16[256,256]{1,0:T(8,128)(2,1)S(1)}, u32[]{:S(2)}, u32[]{:S(2)}) %collective-permute-start.9) | collective-permute-done | bytes 131104 | tf_op jit(solution)/shard_map/ppermute | solution.py:121
  150.1 4.5 %down.1 = bf16[2,256,448]{2,1,0:T(8,128)(2,1)} custom-call(s32[2]{0:T(128)} %pad_add_fusion.half_ref.place_ref, bf16[256,256]{1,0:T(8,128)(2,1)} %gate_up.1.h0_ref, bf16[256,256]{1,0:T(8,128)(2,1)S(1)} %collective-permute-done.3.h1, bf16[256,256]{1,0:T(8,128)(2,1)S(1)} %collective-permute-done.4.h2, bf16[256,256]{1,0:T(8,128)(2,1)S(1)} %collective-permute-done.5.h3, ...), custom_call_target="tpu_custom_call" | custom-call | tf_op jit(solution)/shard_map/down/pallas_call | solution.py:101
  154.7 16.6 %all_to_all.15 = bf16[32,16,448]{2,1,0:T(8,128)(2,1)S(1)} all-to-all(bf16[32,16,448]{2,1,0:T(8,128)(2,1)} %bitcast.27), channel_id=1, replica_groups=mesh['x'=4,'y'=4,'c'=2,'zh'=8,'zl'=2] {'zl','x','y'}, dimensions={0} | all-to-all | bytes 917504 | tf_op jit(solution)/shard_map/all_to_all | solution.py:169
  171.2 0.7 bitcast_reduce_fusion
  (4 shorter events, 0.0 us)
Async XLA Ops:
  1.5 29.5 %all-to-all-start = ((bf16[16,16,448]{2,1,0:T(8,128)(2,1)}), bf16[16,16,448]{2,1,0:T(8,128)(2,1)S(1)}, u32[]{:S(2)}, u32[]{:S(2)}) async-start(bf16[16,16,448]{2,1,0:T(8,128)(2,1)} %bitcast.3), calls=%async_computation | async-start | bytes 524288 | tf_op jit(solution)/shard_map/all_to_all | solution.py:161
  17.2 52.5 %collective-permute-start = (bf16[7168,128]{1,0:T(8,128)(2,1)}, bf16[7168,128]{1,0:T(8,128)(2,1)}, u32[]{:S(2)}, u32[]{:S(2)}) collective-permute-start(bf16[7168,128]{1,0:T(8,128)(2,1)} %bitcast.28), channel_id=1, source_target_pairs={{0,1},{1,0},{2,3},{3,2},{4,5},{5,4},{6,7},{7,6},{8,9},{9,8},{10,11... | collective-permute-start | bytes 5505032 | tf_op jit(solution)/shard_map/ppermute | solution.py:155
  34.0 6.9 %copy-start = (bf16[1,7168,128]{2,1,0:T(8,128)(2,1)S(1)}, bf16[1,7168,128]{2,1,0:T(8,128)(2,1)}, u32[]{:S(2)}) copy-start(bf16[1,7168,128]{2,1,0:T(8,128)(2,1)} %param.8) | copy-start | bytes 5505028
  34.0 66.6 %all-to-all-start.1 = ((bf16[16,16,7296]{2,1,0:T(8,128)(2,1)}), bf16[16,16,7296]{2,1,0:T(8,128)(2,1)}, u32[]{:S(2)}, u32[]{:S(2)}) async-start(bf16[16,16,7296]{2,1,0:T(8,128)(2,1)} %fusion.1), calls=%async_computation.1 | async-start | bytes 7471104 | tf_op jit(solution)/shard_map/all_to_all | solution.py:165
  40.9 59.6 %collective-permute-start.1 = (bf16[7168,128]{1,0:T(8,128)(2,1)S(1)}, bf16[7168,128]{1,0:T(8,128)(2,1)}, u32[]{:S(2)}, u32[]{:S(2)}) collective-permute-start(bf16[7168,128]{1,0:T(8,128)(2,1)S(1)} %bitcast.30), channel_id=1, source_target_pairs={{0,16},{16,0},{1,17},{17,1},{2,18},{18,2},{3,19},{19,3},{4,20},{20... | collective-permute-start | bytes 5505032 | tf_op jit(solution)/shard_map/ppermute | solution.py:153
  69.7 30.8 %collective-permute-start.2 = (bf16[7168,128]{1,0:T(8,128)(2,1)}, bf16[7168,128]{1,0:T(8,128)(2,1)}, u32[]{:S(2)}, u32[]{:S(2)}) collective-permute-start(bf16[7168,128]{1,0:T(8,128)(2,1)} %collective-permute-done.wa1_ref), channel_id=1, source_target_pairs={{0,16},{16,0},{1,17},{17,1},{2,18},{18,2},{3,19},{19,3},{4,20},{20... | collective-permute-start | bytes 5505032 | tf_op jit(solution)/shard_map/ppermute | solution.py:157
  73.0 24.1 %collective-permute-start.11 = (bf16[448,1024]{1,0:T(8,128)(2,1)}, bf16[448,1024]{1,0:T(8,128)(2,1)}, u32[]{:S(2)}, u32[]{:S(2)}) collective-permute-start(bf16[448,1024]{1,0:T(8,128)(2,1)} %bitcast.15.da0_ref), channel_id=1, source_target_pairs={{0,1},{1,0},{2,3},{3,2},{4,5},{5,4},{6,7},{7,6},{8,9},{9,8},{10,11... | collective-permute-start | bytes 2752520 | tf_op jit(solution)/shard_map/ppermute | solution.py:156
  75.0 66.2 %collective-permute-start.10 = (bf16[448,1024]{1,0:T(8,128)(2,1)}, bf16[448,1024]{1,0:T(8,128)(2,1)}, u32[]{:S(2)}, u32[]{:S(2)}) collective-permute-start(bf16[448,1024]{1,0:T(8,128)(2,1)} %bitcast.15.da0_ref), channel_id=1, source_target_pairs={{0,16},{16,0},{1,17},{17,1},{2,18},{18,2},{3,19},{19,3},{4,20},{20... | collective-permute-start | bytes 2752520 | tf_op jit(solution)/shard_map/ppermute | solution.py:154
  97.2 44.1 %collective-permute-start.12 = (bf16[448,1024]{1,0:T(8,128)(2,1)}, bf16[448,1024]{1,0:T(8,128)(2,1)S(1)}, u32[]{:S(2)}, u32[]{:S(2)}) collective-permute-start(bf16[448,1024]{1,0:T(8,128)(2,1)} %collective-permute-done.11.da1_ref), channel_id=1, source_target_pairs={{0,16},{16,0},{1,17},{17,1},{2,18},{18,2},{3,19},{19,3},{4,20},{20... | collective-permute-start | bytes 2752520 | tf_op jit(solution)/shard_map/ppermute | solution.py:158
  106.9 9.4 %collective-permute-start.3 = (bf16[256,256]{1,0:T(8,128)(2,1)}, bf16[256,256]{1,0:T(8,128)(2,1)S(1)}, u32[]{:S(2)}, u32[]{:S(2)}) collective-permute-start(bf16[256,256]{1,0:T(8,128)(2,1)} %gate_up.1.h0_ref), channel_id=1, source_target_pairs={{0,2},{2,4},{4,6},{6,8},{8,10},{10,12},{12,14},{14,0},{1,3},{3,5},... | collective-permute-start | bytes 393224 | tf_op jit(solution)/shard_map/ppermute | solution.py:121
  111.0 12.0 %collective-permute-start.4 = (bf16[256,256]{1,0:T(8,128)(2,1)}, bf16[256,256]{1,0:T(8,128)(2,1)S(1)}, u32[]{:S(2)}, u32[]{:S(2)}) collective-permute-start(bf16[256,256]{1,0:T(8,128)(2,1)} %gate_up.1.h0_ref), channel_id=1, source_target_pairs={{0,14},{2,0},{4,2},{6,4},{8,6},{10,8},{12,10},{14,12},{1,15},{3,1}... | collective-permute-start | bytes 393224 | tf_op jit(solution)/shard_map/ppermute | solution.py:124
  116.3 10.2 %collective-permute-start.5 = (bf16[256,256]{1,0:T(8,128)(2,1)S(1)}, bf16[256,256]{1,0:T(8,128)(2,1)S(1)}, u32[]{:S(2)}, u32[]{:S(2)}) collective-permute-start(bf16[256,256]{1,0:T(8,128)(2,1)S(1)} %collective-permute-done.3.h1), channel_id=1, source_target_pairs={{0,2},{2,4},{4,6},{6,8},{8,10},{10,12},{12,14},{14,0},{1,3},{3,5},... | collective-permute-start | bytes 393224 | tf_op jit(solution)/shard_map/ppermute | solution.py:121
  123.0 11.8 %collective-permute-start.6 = (bf16[256,256]{1,0:T(8,128)(2,1)S(1)}, bf16[256,256]{1,0:T(8,128)(2,1)S(1)}, u32[]{:S(2)}, u32[]{:S(2)}) collective-permute-start(bf16[256,256]{1,0:T(8,128)(2,1)S(1)} %collective-permute-done.4.h2), channel_id=1, source_target_pairs={{0,14},{2,0},{4,2},{6,4},{8,6},{10,8},{12,10},{14,12},{1,15},{3,1}... | collective-permute-start | bytes 393224 | tf_op jit(solution)/shard_map/ppermute | solution.py:124
  126.5 11.8 %collective-permute-start.7 = (bf16[256,256]{1,0:T(8,128)(2,1)S(1)}, bf16[256,256]{1,0:T(8,128)(2,1)S(1)}, u32[]{:S(2)}, u32[]{:S(2)}) collective-permute-start(bf16[256,256]{1,0:T(8,128)(2,1)S(1)} %collective-permute-done.5.h3), channel_id=1, source_target_pairs={{0,2},{2,4},{4,6},{6,8},{8,10},{10,12},{12,14},{14,0},{1,3},{3,5},... | collective-permute-start | bytes 393224 | tf_op jit(solution)/shard_map/ppermute | solution.py:121
  134.8 9.8 %collective-permute-start.8 = (bf16[256,256]{1,0:T(8,128)(2,1)S(1)}, bf16[256,256]{1,0:T(8,128)(2,1)S(1)}, u32[]{:S(2)}, u32[]{:S(2)}) collective-permute-start(bf16[256,256]{1,0:T(8,128)(2,1)S(1)} %collective-permute-done.6.h4), channel_id=1, source_target_pairs={{0,14},{2,0},{4,2},{6,4},{8,6},{10,8},{12,10},{14,12},{1,15},{3,1}... | collective-permute-start | bytes 393224 | tf_op jit(solution)/shard_map/ppermute | solution.py:124
  138.4 11.7 %collective-permute-start.9 = (bf16[256,256]{1,0:T(8,128)(2,1)S(1)}, bf16[256,256]{1,0:T(8,128)(2,1)S(1)}, u32[]{:S(2)}, u32[]{:S(2)}) collective-permute-start(bf16[256,256]{1,0:T(8,128)(2,1)S(1)} %collective-permute-done.7.h5), channel_id=1, source_target_pairs={{0,2},{2,4},{4,6},{6,8},{8,10},{10,12},{12,14},{14,0},{1,3},{3,5},... | collective-permute-start | bytes 393224 | tf_op jit(solution)/shard_map/ppermute | solution.py:121

commit v3 on v2

--- a/solution.py
+++ b/solution.py
@@ -54,7 +54,7 @@
         gate_up_kernel,
         in_specs=[pl.BlockSpec(memory_space=pltpu.SMEM)] + [pl.BlockSpec(memory_space=pl.ANY)] * 5,
         out_specs=pl.BlockSpec(memory_space=pltpu.VMEM),
-        out_shape=jax.ShapeDtypeStruct((count, 256), jnp.bfloat16),
+        out_shape=pltpu.VMEM((count, 256), jnp.bfloat16),
         scratch_shapes=[
             pltpu.VMEM((count, depth), jnp.bfloat16),
             pltpu.VMEM((depth, 512), jnp.bfloat16),
@@ -65,14 +65,12 @@
     )(half, rows, wa0, wa1, wb0, wb1)
 
 
-def down_kernel(place_ref, h0_ref, h1, h2, h3, h4, h5, h6, h7, rows_ref, da0_ref, db0_ref, da1_ref, db1_ref, out_ref, d_buf, h_buf, tail_buf, sems):
+def down_kernel(place_ref, h0, h1, h2, h3, h4, h5, h6, h7, rows_ref, da0_ref, db0_ref, da1_ref, db1_ref, out_ref, d_buf, tail_buf, sems):
     copies = [pltpu.make_async_copy(ref, d_buf.at[i], sems.at[i]) for i, ref in enumerate((da0_ref, db0_ref, da1_ref))]
-    own_copy = pltpu.make_async_copy(h0_ref, h_buf, sems.at[3])
-    tail_copy = pltpu.make_async_copy(rows_ref.at[:, pl.ds(rows_ref.shape[1] - PAD, PAD)], tail_buf, sems.at[4])
-    for copy in (own_copy, tail_copy, *copies):
+    tail_copy = pltpu.make_async_copy(rows_ref.at[:, pl.ds(rows_ref.shape[1] - PAD, PAD)], tail_buf, sems.at[3])
+    for copy in (tail_copy, *copies):
         copy.start()
-    own_copy.wait()
-    parts = (h_buf, h1, h2, h3, h4, h5, h6, h7)
+    parts = (h0, h1, h2, h3, h4, h5, h6, h7)
     hidden = [jnp.concatenate([part[:, 128 * e : 128 * e + 128] for part in parts], axis=1) for e in range(2)]
     starts = [pl.multiple_of(lax.rem(place_ref[1] + by, 8) * 128, 128) for by in HOPS]
     tail_copy.wait()
@@ -97,17 +95,16 @@
 def down(place, parts, rows, da0, db0, da1, db1):
     count, width = parts[0].shape[0], da0.shape[0]
     vmem, anywhere = pl.BlockSpec(memory_space=pltpu.VMEM), pl.BlockSpec(memory_space=pl.ANY)
-    *parts, db1 = [parts[0]] + [pltpu.with_memory_space_constraint(a, pltpu.VMEM) for a in (*parts[1:], db1)]
+    *parts, db1 = [pltpu.with_memory_space_constraint(a, pltpu.VMEM) for a in (*parts, db1)]
     return pl.pallas_call(
         down_kernel,
-        in_specs=[pl.BlockSpec(memory_space=pltpu.SMEM)] + [anywhere] + [vmem] * 7 + [anywhere] * 4 + [vmem],
+        in_specs=[pl.BlockSpec(memory_space=pltpu.SMEM)] + [vmem] * 8 + [anywhere] * 4 + [vmem],
         out_specs=vmem,
         out_shape=jax.ShapeDtypeStruct((2, count, width), jnp.bfloat16),
         scratch_shapes=[
             pltpu.VMEM((3, width, da0.shape[1]), jnp.bfloat16),
-            pltpu.VMEM((count, 256), jnp.bfloat16),
             pltpu.VMEM((count, PAD), jnp.bfloat16),
-            pltpu.SemaphoreType.DMA((5,)),
+            pltpu.SemaphoreType.DMA((4,)),
         ],
         name="down",
     )(place, *parts, rows, da0, db0, da1, db1)

time: 173 us -> 173 us (level)
  transfers between devices with their start and end apart: 15 -> 15, of which waited for: 8 -> 8; matrix products, arithmetic and copies ran while one was open for 3% -> 3% of each run, Pallas kernels for 4% -> 3%
where the time goes in v3:
time: 173 us; the launch traced here: 171 us
  starting transfers between devices  69.4 us (40%)
  waiting for transfers between devices  66.6 us (38%)
  blocking collectives  16.6 us (10%)
  Pallas kernels  10.2 us (6%)
  other arithmetic  5.26 us (3%)
  local copies, waits for them, and re-layouts  2.73 us (2%)
    ppermute x1, waiting for transfers between devices, layer(): wa1 = lax.ppermute(w_in, 'zl', swap)  21 us
    ppermute x1, waiting for transfers between devices, layer(): da1 = lax.ppermute(w_down, 'zl', swap)  20 us
    all_to_all x1, blocking collectives, layer(): lax.all_to_all(out.reshape(32, rows, feats), ('zl',) + XY, 0, 0, tiled=True)  16.6 us
    all_to_all x1, starting transfers between devices, layer(): lax.all_to_all(pieces.reshape(16, rows, feats), ('zh', 'zl'), 0, 0, tiled...  15.7 us
    ppermute x4, starting transfers between devices, ring_gather(): ahead = lax.ppermute(ahead, 'zh', left)  15.2 us
    ppermute x3, starting transfers between devices, ring_gather(): behind = lax.ppermute(behind, 'zh', right)  10.3 us
    ppermute x3, waiting for transfers between devices, ring_gather(): behind = lax.ppermute(behind, 'zh', right)  10.1 us
    all_to_all x1, waiting for transfers between devices, layer(): lax.all_to_all(pieces.reshape(16, rows, feats), ('zh', 'zl'), 0, 0, tiled...  8.24 us
  transfers between devices with their start and end apart: 15, of which 8 were waited for; matrix products, arithmetic and copies ran while one was open for 3% of the time, Pallas kernels for 3%

profile of v3, /device:TPU:1, one launch (start us, length us, event | category | flops | bytes accessed | tf_op | source)
XLA Modules:
  0.0 171.0 jit_solution(11845682852891824646)
XLA Ops:
  0.0 1.5 broadcast_in_dim.30
  1.5 15.7 %all-to-all-start = ((bf16[16,16,448]{2,1,0:T(8,128)(2,1)}), bf16[16,16,448]{2,1,0:T(8,128)(2,1)S(1)}, u32[]{:S(2)}, u32[]{:S(2)}) async-start(bf16[16,16,448]{2,1,0:T(8,128)(2,1)} %bitcast.3), calls=%async_computation | async-start | bytes 524288 | tf_op jit(solution)/shard_map/all_to_all | solution.py:158
  17.2 3.3 %collective-permute-start = (bf16[7168,128]{1,0:T(8,128)(2,1)}, bf16[7168,128]{1,0:T(8,128)(2,1)}, u32[]{:S(2)}, u32[]{:S(2)}) collective-permute-start(bf16[7168,128]{1,0:T(8,128)(2,1)} %bitcast.28), channel_id=1, source_target_pairs={{0,1},{1,0},{2,3},{3,2},{4,5},{5,4},{6,7},{7,6},{8,9},{9,8},{10,11... | collective-permute-start | bytes 5505032 | tf_op jit(solution)/shard_map/ppermute | solution.py:152
  20.5 0.8 slice_select_fusion.1
  21.3 0.1 copy.40
  21.4 0.8 slice_select_fusion
  22.2 0.1 copy.41
  22.3 0.1 select_reduce_fusion
  22.4 0.1 copy.42
  22.6 0.2 copy.47
  22.8 8.2 %all-to-all-done = bf16[16,16,448]{2,1,0:T(8,128)(2,1)S(1)} async-done(((bf16[16,16,448]{2,1,0:T(8,128)(2,1)}), bf16[16,16,448]{2,1,0:T(8,128)(2,1)S(1)}, u32[]{:S(2)}, u32[]{:S(2)}) %all-to-all-start) | async-done | bytes 229408 | tf_op jit(solution)/shard_map/all_to_all | solution.py:158
  31.0 0.1 copy.39
  31.1 0.3 broadcast_in_dim.31
  31.4 0.4 broadcast_in_dim.32
  31.8 2.2 %fusion.1 = bf16[16,16,7296]{2,1,0:T(8,128)(2,1)} fusion(bf16[16,16,6]{2,1,0:T(8,128)(2,1)S(1)} %copy.47, bf16[16,16,7168]{2,1,0:T(8,128)(2,1)S(1)} %broadcast_in_dim.32), kind=kLoop, calls=%fused_computation.2 | loop fusion | flops 11206656 | bytes 7408640 | tf_op jit(solution)/shard_map/concatenate | solution.py:161
  34.0 0.0 copy-start
  34.0 6.9 %all-to-all-start.1 = ((bf16[16,16,7296]{2,1,0:T(8,128)(2,1)}), bf16[16,16,7296]{2,1,0:T(8,128)(2,1)}, u32[]{:S(2)}, u32[]{:S(2)}) async-start(bf16[16,16,7296]{2,1,0:T(8,128)(2,1)} %fusion.1), calls=%async_computation.1 | async-start | bytes 7471104 | tf_op jit(solution)/shard_map/all_to_all | solution.py:162
  40.9 0.0 copy-done
  40.9 7.8 %collective-permute-start.1 = (bf16[7168,128]{1,0:T(8,128)(2,1)S(1)}, bf16[7168,128]{1,0:T(8,128)(2,1)}, u32[]{:S(2)}, u32[]{:S(2)}) collective-permute-start(bf16[7168,128]{1,0:T(8,128)(2,1)S(1)} %bitcast.30), channel_id=1, source_target_pairs={{0,16},{16,0},{1,17},{17,1},{2,18},{18,2},{3,19},{19,3},{4,20},{20... | collective-permute-start | bytes 5505032 | tf_op jit(solution)/shard_map/ppermute | solution.py:150
  48.7 21.0 %collective-permute-done.wa1_ref = bf16[7168,128]{1,0:T(8,128)(2,1)} collective-permute-done((bf16[7168,128]{1,0:T(8,128)(2,1)}, bf16[7168,128]{1,0:T(8,128)(2,1)}, u32[]{:S(2)}, u32[]{:S(2)}) %collective-permute-start) | collective-permute-done | bytes 1835040 | tf_op jit(solution)/shard_map/ppermute | solution.py:152
  69.7 3.3 %collective-permute-start.2 = (bf16[7168,128]{1,0:T(8,128)(2,1)}, bf16[7168,128]{1,0:T(8,128)(2,1)}, u32[]{:S(2)}, u32[]{:S(2)}) collective-permute-start(bf16[7168,128]{1,0:T(8,128)(2,1)} %collective-permute-done.wa1_ref), channel_id=1, source_target_pairs={{0,16},{16,0},{1,17},{17,1},{2,18},{18,2},{3,19},{19,3},{4,20},{20... | collective-permute-start | bytes 5505032 | tf_op jit(solution)/shard_map/ppermute | solution.py:154
  73.0 1.9 %collective-permute-start.11 = (bf16[448,1024]{1,0:T(8,128)(2,1)}, bf16[448,1024]{1,0:T(8,128)(2,1)}, u32[]{:S(2)}, u32[]{:S(2)}) collective-permute-start(bf16[448,1024]{1,0:T(8,128)(2,1)} %bitcast.15.da0_ref), channel_id=1, source_target_pairs={{0,1},{1,0},{2,3},{3,2},{4,5},{5,4},{6,7},{7,6},{8,9},{9,8},{10,11... | collective-permute-start | bytes 2752520 | tf_op jit(solution)/shard_map/ppermute | solution.py:153
  75.0 2.2 %collective-permute-start.10 = (bf16[448,1024]{1,0:T(8,128)(2,1)}, bf16[448,1024]{1,0:T(8,128)(2,1)}, u32[]{:S(2)}, u32[]{:S(2)}) collective-permute-start(bf16[448,1024]{1,0:T(8,128)(2,1)} %bitcast.15.da0_ref), channel_id=1, source_target_pairs={{0,16},{16,0},{1,17},{17,1},{2,18},{18,2},{3,19},{19,3},{4,20},{20... | collective-permute-start | bytes 2752520 | tf_op jit(solution)/shard_map/ppermute | solution.py:151
  77.1 20.0 %collective-permute-done.11.da1_ref = bf16[448,1024]{1,0:T(8,128)(2,1)} collective-permute-done((bf16[448,1024]{1,0:T(8,128)(2,1)}, bf16[448,1024]{1,0:T(8,128)(2,1)}, u32[]{:S(2)}, u32[]{:S(2)}) %collective-permute-start.11) | collective-permute-done | bytes 917536 | tf_op jit(solution)/shard_map/ppermute | solution.py:153
  97.2 2.8 %collective-permute-start.12 = (bf16[448,1024]{1,0:T(8,128)(2,1)}, bf16[448,1024]{1,0:T(8,128)(2,1)S(1)}, u32[]{:S(2)}, u32[]{:S(2)}) collective-permute-start(bf16[448,1024]{1,0:T(8,128)(2,1)} %collective-permute-done.11.da1_ref), channel_id=1, source_target_pairs={{0,16},{16,0},{1,17},{17,1},{2,18},{18,2},{3,19},{19,3},{4,20},{20... | collective-permute-start | bytes 2752520 | tf_op jit(solution)/shard_map/ppermute | solution.py:155
  99.9 0.6 pad_add_fusion.half_ref.place_ref
  100.5 0.0 collective-permute-done.1.wb0_ref
  100.5 0.0 collective-permute-done.2.wb1_ref
  100.5 0.0 all-to-all-done.1
  100.6 5.7 %gate_up.1.h0 = bf16[256,256]{1,0:T(8,128)(2,1)S(1)} custom-call(s32[2]{0:T(128)} %pad_add_fusion.half_ref.place_ref, bf16[256,7296]{1,0:T(8,128)(2,1)} %bitcast.12.rows_ref, bf16[7168,128]{1,0:T(8,128)(2,1)} %bitcast.29, bf16[7168,128]{1,0:T(8,128)(2,1)} %collective-permute-done.wa1_ref, bf16[7168,128]{1,0:T(8,128)(2,1)} %collective-permute-done.1.wb0_ref, ...), custom_call_target="tpu_custom_call" | custom-call | tf_op jit(solution)/shard_map/gate_up/pallas_call | solution.py:53
  106.3 4.1 %collective-permute-start.3 = (bf16[256,256]{1,0:T(8,128)(2,1)S(1)}, bf16[256,256]{1,0:T(8,128)(2,1)S(1)}, u32[]{:S(2)}, u32[]{:S(2)}) collective-permute-start(bf16[256,256]{1,0:T(8,128)(2,1)S(1)} %gate_up.1.h0), channel_id=1, source_target_pairs={{0,2},{2,4},{4,6},{6,8},{8,10},{10,12},{12,14},{14,0},{1,3},{3,5},... | collective-permute-start | bytes 393224 | tf_op jit(solution)/shard_map/ppermute | solution.py:118
  110.4 3.3 %collective-permute-start.4 = (bf16[256,256]{1,0:T(8,128)(2,1)S(1)}, bf16[256,256]{1,0:T(8,128)(2,1)S(1)}, u32[]{:S(2)}, u32[]{:S(2)}) collective-permute-start(bf16[256,256]{1,0:T(8,128)(2,1)S(1)} %gate_up.1.h0), channel_id=1, source_target_pairs={{0,14},{2,0},{4,2},{6,4},{8,6},{10,8},{12,10},{14,12},{1,15},{3,1}... | collective-permute-start | bytes 393224 | tf_op jit(solution)/shard_map/ppermute | solution.py:121
  113.7 1.8 %collective-permute-done.3.h1 = bf16[256,256]{1,0:T(8,128)(2,1)S(1)} collective-permute-done((bf16[256,256]{1,0:T(8,128)(2,1)S(1)}, bf16[256,256]{1,0:T(8,128)(2,1)S(1)}, u32[]{:S(2)}, u32[]{:S(2)}) %collective-permute-start.3) | collective-permute-done | bytes 131104 | tf_op jit(solution)/shard_map/ppermute | solution.py:118
  115.4 4.5 %collective-permute-start.5 = (bf16[256,256]{1,0:T(8,128)(2,1)S(1)}, bf16[256,256]{1,0:T(8,128)(2,1)S(1)}, u32[]{:S(2)}, u32[]{:S(2)}) collective-permute-start(bf16[256,256]{1,0:T(8,128)(2,1)S(1)} %collective-permute-done.3.h1), channel_id=1, source_target_pairs={{0,2},{2,4},{4,6},{6,8},{8,10},{10,12},{12,14},{14,0},{1,3},{3,5},... | collective-permute-start | bytes 393224 | tf_op jit(solution)/shard_map/ppermute | solution.py:118
  119.9 2.2 %collective-permute-done.4.h2 = bf16[256,256]{1,0:T(8,128)(2,1)S(1)} collective-permute-done((bf16[256,256]{1,0:T(8,128)(2,1)S(1)}, bf16[256,256]{1,0:T(8,128)(2,1)S(1)}, u32[]{:S(2)}, u32[]{:S(2)}) %collective-permute-start.4) | collective-permute-done | bytes 131104 | tf_op jit(solution)/shard_map/ppermute | solution.py:121
  122.1 3.5 %collective-permute-start.6 = (bf16[256,256]{1,0:T(8,128)(2,1)S(1)}, bf16[256,256]{1,0:T(8,128)(2,1)S(1)}, u32[]{:S(2)}, u32[]{:S(2)}) collective-permute-start(bf16[256,256]{1,0:T(8,128)(2,1)S(1)} %collective-permute-done.4.h2), channel_id=1, source_target_pairs={{0,14},{2,0},{4,2},{6,4},{8,6},{10,8},{12,10},{14,12},{1,15},{3,1}... | collective-permute-start | bytes 393224 | tf_op jit(solution)/shard_map/ppermute | solution.py:121
  125.7 0.0 collective-permute-done.5.h3
  125.7 3.8 %collective-permute-start.7 = (bf16[256,256]{1,0:T(8,128)(2,1)S(1)}, bf16[256,256]{1,0:T(8,128)(2,1)S(1)}, u32[]{:S(2)}, u32[]{:S(2)}) collective-permute-start(bf16[256,256]{1,0:T(8,128)(2,1)S(1)} %collective-permute-done.5.h3), channel_id=1, source_target_pairs={{0,2},{2,4},{4,6},{6,8},{8,10},{10,12},{12,14},{14,0},{1,3},{3,5},... | collective-permute-start | bytes 393224 | tf_op jit(solution)/shard_map/ppermute | solution.py:118
  129.5 4.5 %collective-permute-done.6.h4 = bf16[256,256]{1,0:T(8,128)(2,1)S(1)} collective-permute-done((bf16[256,256]{1,0:T(8,128)(2,1)S(1)}, bf16[256,256]{1,0:T(8,128)(2,1)S(1)}, u32[]{:S(2)}, u32[]{:S(2)}) %collective-permute-start.6) | collective-permute-done | bytes 131104 | tf_op jit(solution)/shard_map/ppermute | solution.py:121
  134.0 3.5 %collective-permute-start.8 = (bf16[256,256]{1,0:T(8,128)(2,1)S(1)}, bf16[256,256]{1,0:T(8,128)(2,1)S(1)}, u32[]{:S(2)}, u32[]{:S(2)}) collective-permute-start(bf16[256,256]{1,0:T(8,128)(2,1)S(1)} %collective-permute-done.6.h4), channel_id=1, source_target_pairs={{0,14},{2,0},{4,2},{6,4},{8,6},{10,8},{12,10},{14,12},{1,15},{3,1}... | collective-permute-start | bytes 393224 | tf_op jit(solution)/shard_map/ppermute | solution.py:121
  137.5 0.0 collective-permute-done.7.h5
  137.5 2.8 %collective-permute-start.9 = (bf16[256,256]{1,0:T(8,128)(2,1)S(1)}, bf16[256,256]{1,0:T(8,128)(2,1)S(1)}, u32[]{:S(2)}, u32[]{:S(2)}) collective-permute-start(bf16[256,256]{1,0:T(8,128)(2,1)S(1)} %collective-permute-done.7.h5), channel_id=1, source_target_pairs={{0,2},{2,4},{4,6},{6,8},{8,10},{10,12},{12,14},{14,0},{1,3},{3,5},... | collective-permute-start | bytes 393224 | tf_op jit(solution)/shard_map/ppermute | solution.py:118
  140.3 0.0 collective-permute-done.10.db0_ref
  140.4 0.0 collective-permute-done.12.db1_ref
  140.4 3.4 %collective-permute-done.8.h6 = bf16[256,256]{1,0:T(8,128)(2,1)S(1)} collective-permute-done((bf16[256,256]{1,0:T(8,128)(2,1)S(1)}, bf16[256,256]{1,0:T(8,128)(2,1)S(1)}, u32[]{:S(2)}, u32[]{:S(2)}) %collective-permute-start.8) | collective-permute-done | bytes 131104 | tf_op jit(solution)/shard_map/ppermute | solution.py:121
  143.8 5.5 %collective-permute-done.9.h7 = bf16[256,256]{1,0:T(8,128)(2,1)S(1)} collective-permute-done((bf16[256,256]{1,0:T(8,128)(2,1)S(1)}, bf16[256,256]{1,0:T(8,128)(2,1)S(1)}, u32[]{:S(2)}, u32[]{:S(2)}) %collective-permute-start.9) | collective-permute-done | bytes 131104 | tf_op jit(solution)/shard_map/ppermute | solution.py:118
  149.2 4.5 %down.1 = bf16[2,256,448]{2,1,0:T(8,128)(2,1)} custom-call(s32[2]{0:T(128)} %pad_add_fusion.half_ref.place_ref, bf16[256,256]{1,0:T(8,128)(2,1)S(1)} %gate_up.1.h0, bf16[256,256]{1,0:T(8,128)(2,1)S(1)} %collective-permute-done.3.h1, bf16[256,256]{1,0:T(8,128)(2,1)S(1)} %collective-permute-done.4.h2, bf16[256,256]{1,0:T(8,128)(2,1)S(1)} %collective-permute-done.5.h3, ...), custom_call_target="tpu_custom_call" | custom-call | tf_op jit(solution)/shard_map/down/pallas_call | solution.py:99
  153.7 16.6 %all_to_all.15 = bf16[32,16,448]{2,1,0:T(8,128)(2,1)S(1)} all-to-all(bf16[32,16,448]{2,1,0:T(8,128)(2,1)} %bitcast.27), channel_id=1, replica_groups=mesh['x'=4,'y'=4,'c'=2,'zh'=8,'zl'=2] {'zl','x','y'}, dimensions={0} | all-to-all | bytes 917504 | tf_op jit(solution)/shard_map/all_to_all | solution.py:166
  170.3 0.7 bitcast_reduce_fusion
  (4 shorter events, 0.0 us)
Async XLA Ops:
  1.5 29.5 %all-to-all-start = ((bf16[16,16,448]{2,1,0:T(8,128)(2,1)}), bf16[16,16,448]{2,1,0:T(8,128)(2,1)S(1)}, u32[]{:S(2)}, u32[]{:S(2)}) async-start(bf16[16,16,448]{2,1,0:T(8,128)(2,1)} %bitcast.3), calls=%async_computation | async-start | bytes 524288 | tf_op jit(solution)/shard_map/all_to_all | solution.py:158
  17.2 52.5 %collective-permute-start = (bf16[7168,128]{1,0:T(8,128)(2,1)}, bf16[7168,128]{1,0:T(8,128)(2,1)}, u32[]{:S(2)}, u32[]{:S(2)}) collective-permute-start(bf16[7168,128]{1,0:T(8,128)(2,1)} %bitcast.28), channel_id=1, source_target_pairs={{0,1},{1,0},{2,3},{3,2},{4,5},{5,4},{6,7},{7,6},{8,9},{9,8},{10,11... | collective-permute-start | bytes 5505032 | tf_op jit(solution)/shard_map/ppermute | solution.py:152
  34.0 6.9 %copy-start = (bf16[1,7168,128]{2,1,0:T(8,128)(2,1)S(1)}, bf16[1,7168,128]{2,1,0:T(8,128)(2,1)}, u32[]{:S(2)}) copy-start(bf16[1,7168,128]{2,1,0:T(8,128)(2,1)} %param.8) | copy-start | bytes 5505028
  34.0 66.6 %all-to-all-start.1 = ((bf16[16,16,7296]{2,1,0:T(8,128)(2,1)}), bf16[16,16,7296]{2,1,0:T(8,128)(2,1)}, u32[]{:S(2)}, u32[]{:S(2)}) async-start(bf16[16,16,7296]{2,1,0:T(8,128)(2,1)} %fusion.1), calls=%async_computation.1 | async-start | bytes 7471104 | tf_op jit(solution)/shard_map/all_to_all | solution.py:162
  40.9 59.6 %collective-permute-start.1 = (bf16[7168,128]{1,0:T(8,128)(2,1)S(1)}, bf16[7168,128]{1,0:T(8,128)(2,1)}, u32[]{:S(2)}, u32[]{:S(2)}) collective-permute-start(bf16[7168,128]{1,0:T(8,128)(2,1)S(1)} %bitcast.30), channel_id=1, source_target_pairs={{0,16},{16,0},{1,17},{17,1},{2,18},{18,2},{3,19},{19,3},{4,20},{20... | collective-permute-start | bytes 5505032 | tf_op jit(solution)/shard_map/ppermute | solution.py:150
  69.7 30.8 %collective-permute-start.2 = (bf16[7168,128]{1,0:T(8,128)(2,1)}, bf16[7168,128]{1,0:T(8,128)(2,1)}, u32[]{:S(2)}, u32[]{:S(2)}) collective-permute-start(bf16[7168,128]{1,0:T(8,128)(2,1)} %collective-permute-done.wa1_ref), channel_id=1, source_target_pairs={{0,16},{16,0},{1,17},{17,1},{2,18},{18,2},{3,19},{19,3},{4,20},{20... | collective-permute-start | bytes 5505032 | tf_op jit(solution)/shard_map/ppermute | solution.py:154
  73.0 24.1 %collective-permute-start.11 = (bf16[448,1024]{1,0:T(8,128)(2,1)}, bf16[448,1024]{1,0:T(8,128)(2,1)}, u32[]{:S(2)}, u32[]{:S(2)}) collective-permute-start(bf16[448,1024]{1,0:T(8,128)(2,1)} %bitcast.15.da0_ref), channel_id=1, source_target_pairs={{0,1},{1,0},{2,3},{3,2},{4,5},{5,4},{6,7},{7,6},{8,9},{9,8},{10,11... | collective-permute-start | bytes 2752520 | tf_op jit(solution)/shard_map/ppermute | solution.py:153
  75.0 65.4 %collective-permute-start.10 = (bf16[448,1024]{1,0:T(8,128)(2,1)}, bf16[448,1024]{1,0:T(8,128)(2,1)}, u32[]{:S(2)}, u32[]{:S(2)}) collective-permute-start(bf16[448,1024]{1,0:T(8,128)(2,1)} %bitcast.15.da0_ref), channel_id=1, source_target_pairs={{0,16},{16,0},{1,17},{17,1},{2,18},{18,2},{3,19},{19,3},{4,20},{20... | collective-permute-start | bytes 2752520 | tf_op jit(solution)/shard_map/ppermute | solution.py:151
  97.2 43.2 %collective-permute-start.12 = (bf16[448,1024]{1,0:T(8,128)(2,1)}, bf16[448,1024]{1,0:T(8,128)(2,1)S(1)}, u32[]{:S(2)}, u32[]{:S(2)}) collective-permute-start(bf16[448,1024]{1,0:T(8,128)(2,1)} %collective-permute-done.11.da1_ref), channel_id=1, source_target_pairs={{0,16},{16,0},{1,17},{17,1},{2,18},{18,2},{3,19},{19,3},{4,20},{20... | collective-permute-start | bytes 2752520 | tf_op jit(solution)/shard_map/ppermute | solution.py:155
  106.3 9.2 %collective-permute-start.3 = (bf16[256,256]{1,0:T(8,128)(2,1)S(1)}, bf16[256,256]{1,0:T(8,128)(2,1)S(1)}, u32[]{:S(2)}, u32[]{:S(2)}) collective-permute-start(bf16[256,256]{1,0:T(8,128)(2,1)S(1)} %gate_up.1.h0), channel_id=1, source_target_pairs={{0,2},{2,4},{4,6},{6,8},{8,10},{10,12},{12,14},{14,0},{1,3},{3,5},... | collective-permute-start | bytes 393224 | tf_op jit(solution)/shard_map/ppermute | solution.py:118
  110.4 11.8 %collective-permute-start.4 = (bf16[256,256]{1,0:T(8,128)(2,1)S(1)}, bf16[256,256]{1,0:T(8,128)(2,1)S(1)}, u32[]{:S(2)}, u32[]{:S(2)}) collective-permute-start(bf16[256,256]{1,0:T(8,128)(2,1)S(1)} %gate_up.1.h0), channel_id=1, source_target_pairs={{0,14},{2,0},{4,2},{6,4},{8,6},{10,8},{12,10},{14,12},{1,15},{3,1}... | collective-permute-start | bytes 393224 | tf_op jit(solution)/shard_map/ppermute | solution.py:121
  115.4 10.2 %collective-permute-start.5 = (bf16[256,256]{1,0:T(8,128)(2,1)S(1)}, bf16[256,256]{1,0:T(8,128)(2,1)S(1)}, u32[]{:S(2)}, u32[]{:S(2)}) collective-permute-start(bf16[256,256]{1,0:T(8,128)(2,1)S(1)} %collective-permute-done.3.h1), channel_id=1, source_target_pairs={{0,2},{2,4},{4,6},{6,8},{8,10},{10,12},{12,14},{14,0},{1,3},{3,5},... | collective-permute-start | bytes 393224 | tf_op jit(solution)/shard_map/ppermute | solution.py:118
  122.1 11.8 %collective-permute-start.6 = (bf16[256,256]{1,0:T(8,128)(2,1)S(1)}, bf16[256,256]{1,0:T(8,128)(2,1)S(1)}, u32[]{:S(2)}, u32[]{:S(2)}) collective-permute-start(bf16[256,256]{1,0:T(8,128)(2,1)S(1)} %collective-permute-done.4.h2), channel_id=1, source_target_pairs={{0,14},{2,0},{4,2},{6,4},{8,6},{10,8},{12,10},{14,12},{1,15},{3,1}... | collective-permute-start | bytes 393224 | tf_op jit(solution)/shard_map/ppermute | solution.py:121
  125.7 11.8 %collective-permute-start.7 = (bf16[256,256]{1,0:T(8,128)(2,1)S(1)}, bf16[256,256]{1,0:T(8,128)(2,1)S(1)}, u32[]{:S(2)}, u32[]{:S(2)}) collective-permute-start(bf16[256,256]{1,0:T(8,128)(2,1)S(1)} %collective-permute-done.5.h3), channel_id=1, source_target_pairs={{0,2},{2,4},{4,6},{6,8},{8,10},{10,12},{12,14},{14,0},{1,3},{3,5},... | collective-permute-start | bytes 393224 | tf_op jit(solution)/shard_map/ppermute | solution.py:118
  134.0 9.8 %collective-permute-start.8 = (bf16[256,256]{1,0:T(8,128)(2,1)S(1)}, bf16[256,256]{1,0:T(8,128)(2,1)S(1)}, u32[]{:S(2)}, u32[]{:S(2)}) collective-permute-start(bf16[256,256]{1,0:T(8,128)(2,1)S(1)} %collective-permute-done.6.h4), channel_id=1, source_target_pairs={{0,14},{2,0},{4,2},{6,4},{8,6},{10,8},{12,10},{14,12},{1,15},{3,1}... | collective-permute-start | bytes 393224 | tf_op jit(solution)/shard_map/ppermute | solution.py:121
  137.5 11.7 %collective-permute-start.9 = (bf16[256,256]{1,0:T(8,128)(2,1)S(1)}, bf16[256,256]{1,0:T(8,128)(2,1)S(1)}, u32[]{:S(2)}, u32[]{:S(2)}) collective-permute-start(bf16[256,256]{1,0:T(8,128)(2,1)S(1)} %collective-permute-done.7.h5), channel_id=1, source_target_pairs={{0,2},{2,4},{4,6},{6,8},{8,10},{10,12},{12,14},{14,0},{1,3},{3,5},... | collective-permute-start | bytes 393224 | tf_op jit(solution)/shard_map/ppermute | solution.py:118

commit v4 on v3

--- a/solution.py
+++ b/solution.py
@@ -59,14 +59,14 @@
             pltpu.VMEM((count, depth), jnp.bfloat16),
             pltpu.VMEM((depth, 512), jnp.bfloat16),
             pltpu.VMEM((count, 512), jnp.float32),
-            pltpu.SemaphoreType.DMA((7, 5)),
+            pltpu.SemaphoreType.DMA((4, 5)),
         ],
         name="gate_up",
     )(half, rows, wa0, wa1, wb0, wb1)
 
 
 def down_kernel(place_ref, h0, h1, h2, h3, h4, h5, h6, h7, rows_ref, da0_ref, db0_ref, da1_ref, db1_ref, out_ref, d_buf, tail_buf, sems):
-    copies = [pltpu.make_async_copy(ref, d_buf.at[i], sems.at[i]) for i, ref in enumerate((da0_ref, db0_ref, da1_ref))]
+    copies = [pltpu.make_async_copy(ref, d_buf.at[i], sems.at[i]) for i, ref in enumerate((da1_ref, db0_ref, da0_ref))]
     tail_copy = pltpu.make_async_copy(rows_ref.at[:, pl.ds(rows_ref.shape[1] - PAD, PAD)], tail_buf, sems.at[3])
     for copy in (tail_copy, *copies):
         copy.start()
@@ -78,13 +78,13 @@
     weight = [
         tail[:, 3 * e : 3 * e + 1] + tail[:, 3 * e + 1 : 3 * e + 2] + tail[:, 3 * e + 2 : 3 * e + 3] for e in range(2)
     ]
-    for side in range(2):
+    for side in (1, 0):
         total = 0.0
-        for e in range(2):
-            i = 2 * side + e
-            if i < 3:
+        for e in (1, 0):
+            i = 2 * (1 - side) - e
+            if i >= 0:
                 copies[i].wait()
-            d_ref = d_buf.at[i] if i < 3 else db1_ref
+            d_ref = d_buf.at[i] if i >= 0 else db1_ref
             rolled = jnp.concatenate([d_ref[:, pl.ds(start, 128)] for start in starts], axis=1)
             y = lax.dot_general(hidden[e], rolled, (((1,), (1,)), ((), ())), preferred_element_type=jnp.float32)
             total = total + weight[e] * y.astype(jnp.bfloat16).astype(jnp.float32)
@@ -100,7 +100,7 @@
         down_kernel,
         in_specs=[pl.BlockSpec(memory_space=pltpu.SMEM)] + [vmem] * 8 + [anywhere] * 4 + [vmem],
         out_specs=vmem,
-        out_shape=jax.ShapeDtypeStruct((2, count, width), jnp.bfloat16),
+        out_shape=pltpu.VMEM((2, count, width), jnp.bfloat16),
         scratch_shapes=[
             pltpu.VMEM((3, width, da0.shape[1]), jnp.bfloat16),
             pltpu.VMEM((count, PAD), jnp.bfloat16),

time: 173 us -> 171 us (0.988)
  no operation moved by 1% of the time
where the time goes in v4:
time: 171 us; the launch traced here: 170 us
  starting transfers between devices  69.4 us (41%)
  waiting for transfers between devices  66.6 us (39%)
  blocking collectives  16.4 us (10%)
  Pallas kernels  9.26 us (5%)
  other arithmetic  5.24 us (3%)
  local copies, waits for them, and re-layouts  2.73 us (2%)
    ppermute x1, waiting for transfers between devices, layer(): wa1 = lax.ppermute(w_in, 'zl', swap)  21 us
    ppermute x1, waiting for transfers between devices, layer(): da1 = lax.ppermute(w_down, 'zl', swap)  20 us
    all_to_all x1, blocking collectives, layer(): lax.all_to_all(out.reshape(32, rows, feats), ('zl',) + XY, 0, 0, tiled=True)  16.4 us
    all_to_all x1, starting transfers between devices, layer(): lax.all_to_all(pieces.reshape(16, rows, feats), ('zh', 'zl'), 0, 0, tiled...  15.7 us
    ppermute x4, starting transfers between devices, ring_gather(): ahead = lax.ppermute(ahead, 'zh', left)  15.2 us
    ppermute x3, starting transfers between devices, ring_gather(): behind = lax.ppermute(behind, 'zh', right)  10.3 us
    ppermute x3, waiting for transfers between devices, ring_gather(): behind = lax.ppermute(behind, 'zh', right)  10.1 us
    all_to_all x1, waiting for transfers between devices, layer(): lax.all_to_all(pieces.reshape(16, rows, feats), ('zh', 'zl'), 0, 0, tiled...  8.24 us
  transfers between devices with their start and end apart: 15, of which 8 were waited for; matrix products, arithmetic and copies ran while one was open for 3% of the time, Pallas kernels for 3%

profile of v4, /device:TPU:1, one launch (start us, length us, event | category | flops | bytes accessed | tf_op | source)
XLA Modules:
  0.0 169.8 jit_solution(18218447153003733706)
XLA Ops:
  0.0 1.5 broadcast_in_dim.30
  1.5 15.7 %all-to-all-start = ((bf16[16,16,448]{2,1,0:T(8,128)(2,1)}), bf16[16,16,448]{2,1,0:T(8,128)(2,1)S(1)}, u32[]{:S(2)}, u32[]{:S(2)}) async-start(bf16[16,16,448]{2,1,0:T(8,128)(2,1)} %bitcast.3), calls=%async_computation | async-start | bytes 524288 | tf_op jit(solution)/shard_map/all_to_all | solution.py:158
  17.2 3.3 %collective-permute-start = (bf16[7168,128]{1,0:T(8,128)(2,1)}, bf16[7168,128]{1,0:T(8,128)(2,1)}, u32[]{:S(2)}, u32[]{:S(2)}) collective-permute-start(bf16[7168,128]{1,0:T(8,128)(2,1)} %bitcast.28), channel_id=1, source_target_pairs={{0,1},{1,0},{2,3},{3,2},{4,5},{5,4},{6,7},{7,6},{8,9},{9,8},{10,11... | collective-permute-start | bytes 5505032 | tf_op jit(solution)/shard_map/ppermute | solution.py:152
  20.5 0.8 slice_select_fusion.1
  21.3 0.1 copy.40
  21.4 0.8 slice_select_fusion
  22.2 0.1 copy.41
  22.3 0.1 select_reduce_fusion
  22.4 0.1 copy.42
  22.6 0.2 copy.47
  22.8 8.2 %all-to-all-done = bf16[16,16,448]{2,1,0:T(8,128)(2,1)S(1)} async-done(((bf16[16,16,448]{2,1,0:T(8,128)(2,1)}), bf16[16,16,448]{2,1,0:T(8,128)(2,1)S(1)}, u32[]{:S(2)}, u32[]{:S(2)}) %all-to-all-start) | async-done | bytes 229408 | tf_op jit(solution)/shard_map/all_to_all | solution.py:158
  31.0 0.1 copy.39
  31.1 0.3 broadcast_in_dim.31
  31.4 0.4 broadcast_in_dim.32
  31.8 2.2 %fusion.1 = bf16[16,16,7296]{2,1,0:T(8,128)(2,1)} fusion(bf16[16,16,6]{2,1,0:T(8,128)(2,1)S(1)} %copy.47, bf16[16,16,7168]{2,1,0:T(8,128)(2,1)S(1)} %broadcast_in_dim.32), kind=kLoop, calls=%fused_computation.2 | loop fusion | flops 11206656 | bytes 7408640 | tf_op jit(solution)/shard_map/concatenate | solution.py:161
  34.0 0.0 copy-start
  34.0 6.9 %all-to-all-start.1 = ((bf16[16,16,7296]{2,1,0:T(8,128)(2,1)}), bf16[16,16,7296]{2,1,0:T(8,128)(2,1)}, u32[]{:S(2)}, u32[]{:S(2)}) async-start(bf16[16,16,7296]{2,1,0:T(8,128)(2,1)} %fusion.1), calls=%async_computation.1 | async-start | bytes 7471104 | tf_op jit(solution)/shard_map/all_to_all | solution.py:162
  40.9 0.0 copy-done
  40.9 7.8 %collective-permute-start.1 = (bf16[7168,128]{1,0:T(8,128)(2,1)S(1)}, bf16[7168,128]{1,0:T(8,128)(2,1)}, u32[]{:S(2)}, u32[]{:S(2)}) collective-permute-start(bf16[7168,128]{1,0:T(8,128)(2,1)S(1)} %bitcast.30), channel_id=1, source_target_pairs={{0,16},{16,0},{1,17},{17,1},{2,18},{18,2},{3,19},{19,3},{4,20},{20... | collective-permute-start | bytes 5505032 | tf_op jit(solution)/shard_map/ppermute | solution.py:150
  48.7 21.0 %collective-permute-done.wa1_ref = bf16[7168,128]{1,0:T(8,128)(2,1)} collective-permute-done((bf16[7168,128]{1,0:T(8,128)(2,1)}, bf16[7168,128]{1,0:T(8,128)(2,1)}, u32[]{:S(2)}, u32[]{:S(2)}) %collective-permute-start) | collective-permute-done | bytes 1835040 | tf_op jit(solution)/shard_map/ppermute | solution.py:152
  69.7 3.3 %collective-permute-start.2 = (bf16[7168,128]{1,0:T(8,128)(2,1)}, bf16[7168,128]{1,0:T(8,128)(2,1)}, u32[]{:S(2)}, u32[]{:S(2)}) collective-permute-start(bf16[7168,128]{1,0:T(8,128)(2,1)} %collective-permute-done.wa1_ref), channel_id=1, source_target_pairs={{0,16},{16,0},{1,17},{17,1},{2,18},{18,2},{3,19},{19,3},{4,20},{20... | collective-permute-start | bytes 5505032 | tf_op jit(solution)/shard_map/ppermute | solution.py:154
  73.0 1.9 %collective-permute-start.11 = (bf16[448,1024]{1,0:T(8,128)(2,1)}, bf16[448,1024]{1,0:T(8,128)(2,1)}, u32[]{:S(2)}, u32[]{:S(2)}) collective-permute-start(bf16[448,1024]{1,0:T(8,128)(2,1)} %bitcast.15.da0_ref), channel_id=1, source_target_pairs={{0,1},{1,0},{2,3},{3,2},{4,5},{5,4},{6,7},{7,6},{8,9},{9,8},{10,11... | collective-permute-start | bytes 2752520 | tf_op jit(solution)/shard_map/ppermute | solution.py:153
  75.0 2.2 %collective-permute-start.10 = (bf16[448,1024]{1,0:T(8,128)(2,1)}, bf16[448,1024]{1,0:T(8,128)(2,1)}, u32[]{:S(2)}, u32[]{:S(2)}) collective-permute-start(bf16[448,1024]{1,0:T(8,128)(2,1)} %bitcast.15.da0_ref), channel_id=1, source_target_pairs={{0,16},{16,0},{1,17},{17,1},{2,18},{18,2},{3,19},{19,3},{4,20},{20... | collective-permute-start | bytes 2752520 | tf_op jit(solution)/shard_map/ppermute | solution.py:151
  77.1 20.0 %collective-permute-done.11.da1_ref = bf16[448,1024]{1,0:T(8,128)(2,1)} collective-permute-done((bf16[448,1024]{1,0:T(8,128)(2,1)}, bf16[448,1024]{1,0:T(8,128)(2,1)}, u32[]{:S(2)}, u32[]{:S(2)}) %collective-permute-start.11) | collective-permute-done | bytes 917536 | tf_op jit(solution)/shard_map/ppermute | solution.py:153
  97.2 2.8 %collective-permute-start.12 = (bf16[448,1024]{1,0:T(8,128)(2,1)}, bf16[448,1024]{1,0:T(8,128)(2,1)S(1)}, u32[]{:S(2)}, u32[]{:S(2)}) collective-permute-start(bf16[448,1024]{1,0:T(8,128)(2,1)} %collective-permute-done.11.da1_ref), channel_id=1, source_target_pairs={{0,16},{16,0},{1,17},{17,1},{2,18},{18,2},{3,19},{19,3},{4,20},{20... | collective-permute-start | bytes 2752520 | tf_op jit(solution)/shard_map/ppermute | solution.py:155
  99.9 0.6 pad_add_fusion.half_ref.place_ref
  100.5 0.0 collective-permute-done.1.wb0_ref
  100.5 0.0 collective-permute-done.2.wb1_ref
  100.5 0.0 all-to-all-done.1
  100.5 5.8 %gate_up.1.h0 = bf16[256,256]{1,0:T(8,128)(2,1)S(1)} custom-call(s32[2]{0:T(128)} %pad_add_fusion.half_ref.place_ref, bf16[256,7296]{1,0:T(8,128)(2,1)} %bitcast.12.rows_ref, bf16[7168,128]{1,0:T(8,128)(2,1)} %bitcast.29, bf16[7168,128]{1,0:T(8,128)(2,1)} %collective-permute-done.wa1_ref, bf16[7168,128]{1,0:T(8,128)(2,1)} %collective-permute-done.1.wb0_ref, ...), custom_call_target="tpu_custom_call" | custom-call | tf_op jit(solution)/shard_map/gate_up/pallas_call | solution.py:53
  106.3 4.1 %collective-permute-start.3 = (bf16[256,256]{1,0:T(8,128)(2,1)S(1)}, bf16[256,256]{1,0:T(8,128)(2,1)S(1)}, u32[]{:S(2)}, u32[]{:S(2)}) collective-permute-start(bf16[256,256]{1,0:T(8,128)(2,1)S(1)} %gate_up.1.h0), channel_id=1, source_target_pairs={{0,2},{2,4},{4,6},{6,8},{8,10},{10,12},{12,14},{14,0},{1,3},{3,5},... | collective-permute-start | bytes 393224 | tf_op jit(solution)/shard_map/ppermute | solution.py:118
  110.4 3.3 %collective-permute-start.4 = (bf16[256,256]{1,0:T(8,128)(2,1)S(1)}, bf16[256,256]{1,0:T(8,128)(2,1)S(1)}, u32[]{:S(2)}, u32[]{:S(2)}) collective-permute-start(bf16[256,256]{1,0:T(8,128)(2,1)S(1)} %gate_up.1.h0), channel_id=1, source_target_pairs={{0,14},{2,0},{4,2},{6,4},{8,6},{10,8},{12,10},{14,12},{1,15},{3,1}... | collective-permute-start | bytes 393224 | tf_op jit(solution)/shard_map/ppermute | solution.py:121
  113.7 1.8 %collective-permute-done.3.h1 = bf16[256,256]{1,0:T(8,128)(2,1)S(1)} collective-permute-done((bf16[256,256]{1,0:T(8,128)(2,1)S(1)}, bf16[256,256]{1,0:T(8,128)(2,1)S(1)}, u32[]{:S(2)}, u32[]{:S(2)}) %collective-permute-start.3) | collective-permute-done | bytes 131104 | tf_op jit(solution)/shard_map/ppermute | solution.py:118
  115.5 4.5 %collective-permute-start.5 = (bf16[256,256]{1,0:T(8,128)(2,1)S(1)}, bf16[256,256]{1,0:T(8,128)(2,1)S(1)}, u32[]{:S(2)}, u32[]{:S(2)}) collective-permute-start(bf16[256,256]{1,0:T(8,128)(2,1)S(1)} %collective-permute-done.3.h1), channel_id=1, source_target_pairs={{0,2},{2,4},{4,6},{6,8},{8,10},{10,12},{12,14},{14,0},{1,3},{3,5},... | collective-permute-start | bytes 393224 | tf_op jit(solution)/shard_map/ppermute | solution.py:118
  120.0 2.2 %collective-permute-done.4.h2 = bf16[256,256]{1,0:T(8,128)(2,1)S(1)} collective-permute-done((bf16[256,256]{1,0:T(8,128)(2,1)S(1)}, bf16[256,256]{1,0:T(8,128)(2,1)S(1)}, u32[]{:S(2)}, u32[]{:S(2)}) %collective-permute-start.4) | collective-permute-done | bytes 131104 | tf_op jit(solution)/shard_map/ppermute | solution.py:121
  122.2 3.5 %collective-permute-start.6 = (bf16[256,256]{1,0:T(8,128)(2,1)S(1)}, bf16[256,256]{1,0:T(8,128)(2,1)S(1)}, u32[]{:S(2)}, u32[]{:S(2)}) collective-permute-start(bf16[256,256]{1,0:T(8,128)(2,1)S(1)} %collective-permute-done.4.h2), channel_id=1, source_target_pairs={{0,14},{2,0},{4,2},{6,4},{8,6},{10,8},{12,10},{14,12},{1,15},{3,1}... | collective-permute-start | bytes 393224 | tf_op jit(solution)/shard_map/ppermute | solution.py:121
  125.7 0.0 collective-permute-done.5.h3
  125.7 3.8 %collective-permute-start.7 = (bf16[256,256]{1,0:T(8,128)(2,1)S(1)}, bf16[256,256]{1,0:T(8,128)(2,1)S(1)}, u32[]{:S(2)}, u32[]{:S(2)}) collective-permute-start(bf16[256,256]{1,0:T(8,128)(2,1)S(1)} %collective-permute-done.5.h3), channel_id=1, source_target_pairs={{0,2},{2,4},{4,6},{6,8},{8,10},{10,12},{12,14},{14,0},{1,3},{3,5},... | collective-permute-start | bytes 393224 | tf_op jit(solution)/shard_map/ppermute | solution.py:118
  129.6 4.5 %collective-permute-done.6.h4 = bf16[256,256]{1,0:T(8,128)(2,1)S(1)} collective-permute-done((bf16[256,256]{1,0:T(8,128)(2,1)S(1)}, bf16[256,256]{1,0:T(8,128)(2,1)S(1)}, u32[]{:S(2)}, u32[]{:S(2)}) %collective-permute-start.6) | collective-permute-done | bytes 131104 | tf_op jit(solution)/shard_map/ppermute | solution.py:121
  134.0 3.5 %collective-permute-start.8 = (bf16[256,256]{1,0:T(8,128)(2,1)S(1)}, bf16[256,256]{1,0:T(8,128)(2,1)S(1)}, u32[]{:S(2)}, u32[]{:S(2)}) collective-permute-start(bf16[256,256]{1,0:T(8,128)(2,1)S(1)} %collective-permute-done.6.h4), channel_id=1, source_target_pairs={{0,14},{2,0},{4,2},{6,4},{8,6},{10,8},{12,10},{14,12},{1,15},{3,1}... | collective-permute-start | bytes 393224 | tf_op jit(solution)/shard_map/ppermute | solution.py:121
  137.5 0.0 collective-permute-done.7.h5
  137.5 2.8 %collective-permute-start.9 = (bf16[256,256]{1,0:T(8,128)(2,1)S(1)}, bf16[256,256]{1,0:T(8,128)(2,1)S(1)}, u32[]{:S(2)}, u32[]{:S(2)}) collective-permute-start(bf16[256,256]{1,0:T(8,128)(2,1)S(1)} %collective-permute-done.7.h5), channel_id=1, source_target_pairs={{0,2},{2,4},{4,6},{6,8},{8,10},{10,12},{12,14},{14,0},{1,3},{3,5},... | collective-permute-start | bytes 393224 | tf_op jit(solution)/shard_map/ppermute | solution.py:118
  140.4 0.0 collective-permute-done.10.db0_ref
  140.4 0.0 collective-permute-done.12.db1_ref
  140.4 3.4 %collective-permute-done.8.h6 = bf16[256,256]{1,0:T(8,128)(2,1)S(1)} collective-permute-done((bf16[256,256]{1,0:T(8,128)(2,1)S(1)}, bf16[256,256]{1,0:T(8,128)(2,1)S(1)}, u32[]{:S(2)}, u32[]{:S(2)}) %collective-permute-start.8) | collective-permute-done | bytes 131104 | tf_op jit(solution)/shard_map/ppermute | solution.py:121
  143.8 5.5 %collective-permute-done.9.h7 = bf16[256,256]{1,0:T(8,128)(2,1)S(1)} collective-permute-done((bf16[256,256]{1,0:T(8,128)(2,1)S(1)}, bf16[256,256]{1,0:T(8,128)(2,1)S(1)}, u32[]{:S(2)}, u32[]{:S(2)}) %collective-permute-start.9) | collective-permute-done | bytes 131104 | tf_op jit(solution)/shard_map/ppermute | solution.py:118
  149.3 3.5 %down.1 = bf16[2,256,448]{2,1,0:T(8,128)(2,1)S(1)} custom-call(s32[2]{0:T(128)} %pad_add_fusion.half_ref.place_ref, bf16[256,256]{1,0:T(8,128)(2,1)S(1)} %gate_up.1.h0, bf16[256,256]{1,0:T(8,128)(2,1)S(1)} %collective-permute-done.3.h1, bf16[256,256]{1,0:T(8,128)(2,1)S(1)} %collective-permute-done.4.h2, bf16[256,256]{1,0:T(8,128)(2,1)S(1)} %collective-permute-done.5.h3, ...), custom_call_target="tpu_custom_call" | custom-call | tf_op jit(solution)/shard_map/down/pallas_call | solution.py:99
  152.8 16.4 %all_to_all.15 = bf16[32,16,448]{2,1,0:T(8,128)(2,1)S(1)} all-to-all(bf16[32,16,448]{2,1,0:T(8,128)(2,1)S(1)} %bitcast.27), channel_id=1, replica_groups=mesh['x'=4,'y'=4,'c'=2,'zh'=8,'zl'=2] {'zl','x','y'}, dimensions={0} | all-to-all | bytes 917504 | tf_op jit(solution)/shard_map/all_to_all | solution.py:166
  169.1 0.7 bitcast_reduce_fusion
  (4 shorter events, 0.0 us)
Async XLA Ops:
  1.5 29.5 %all-to-all-start = ((bf16[16,16,448]{2,1,0:T(8,128)(2,1)}), bf16[16,16,448]{2,1,0:T(8,128)(2,1)S(1)}, u32[]{:S(2)}, u32[]{:S(2)}) async-start(bf16[16,16,448]{2,1,0:T(8,128)(2,1)} %bitcast.3), calls=%async_computation | async-start | bytes 524288 | tf_op jit(solution)/shard_map/all_to_all | solution.py:158
  17.2 52.5 %collective-permute-start = (bf16[7168,128]{1,0:T(8,128)(2,1)}, bf16[7168,128]{1,0:T(8,128)(2,1)}, u32[]{:S(2)}, u32[]{:S(2)}) collective-permute-start(bf16[7168,128]{1,0:T(8,128)(2,1)} %bitcast.28), channel_id=1, source_target_pairs={{0,1},{1,0},{2,3},{3,2},{4,5},{5,4},{6,7},{7,6},{8,9},{9,8},{10,11... | collective-permute-start | bytes 5505032 | tf_op jit(solution)/shard_map/ppermute | solution.py:152
  34.0 6.9 %copy-start = (bf16[1,7168,128]{2,1,0:T(8,128)(2,1)S(1)}, bf16[1,7168,128]{2,1,0:T(8,128)(2,1)}, u32[]{:S(2)}) copy-start(bf16[1,7168,128]{2,1,0:T(8,128)(2,1)} %param.8) | copy-start | bytes 5505028
  34.0 66.5 %all-to-all-start.1 = ((bf16[16,16,7296]{2,1,0:T(8,128)(2,1)}), bf16[16,16,7296]{2,1,0:T(8,128)(2,1)}, u32[]{:S(2)}, u32[]{:S(2)}) async-start(bf16[16,16,7296]{2,1,0:T(8,128)(2,1)} %fusion.1), calls=%async_computation.1 | async-start | bytes 7471104 | tf_op jit(solution)/shard_map/all_to_all | solution.py:162
  40.9 59.6 %collective-permute-start.1 = (bf16[7168,128]{1,0:T(8,128)(2,1)S(1)}, bf16[7168,128]{1,0:T(8,128)(2,1)}, u32[]{:S(2)}, u32[]{:S(2)}) collective-permute-start(bf16[7168,128]{1,0:T(8,128)(2,1)S(1)} %bitcast.30), channel_id=1, source_target_pairs={{0,16},{16,0},{1,17},{17,1},{2,18},{18,2},{3,19},{19,3},{4,20},{20... | collective-permute-start | bytes 5505032 | tf_op jit(solution)/shard_map/ppermute | solution.py:150
  69.7 30.8 %collective-permute-start.2 = (bf16[7168,128]{1,0:T(8,128)(2,1)}, bf16[7168,128]{1,0:T(8,128)(2,1)}, u32[]{:S(2)}, u32[]{:S(2)}) collective-permute-start(bf16[7168,128]{1,0:T(8,128)(2,1)} %collective-permute-done.wa1_ref), channel_id=1, source_target_pairs={{0,16},{16,0},{1,17},{17,1},{2,18},{18,2},{3,19},{19,3},{4,20},{20... | collective-permute-start | bytes 5505032 | tf_op jit(solution)/shard_map/ppermute | solution.py:154
  73.0 24.1 %collective-permute-start.11 = (bf16[448,1024]{1,0:T(8,128)(2,1)}, bf16[448,1024]{1,0:T(8,128)(2,1)}, u32[]{:S(2)}, u32[]{:S(2)}) collective-permute-start(bf16[448,1024]{1,0:T(8,128)(2,1)} %bitcast.15.da0_ref), channel_id=1, source_target_pairs={{0,1},{1,0},{2,3},{3,2},{4,5},{5,4},{6,7},{7,6},{8,9},{9,8},{10,11... | collective-permute-start | bytes 2752520 | tf_op jit(solution)/shard_map/ppermute | solution.py:153
  75.0 65.4 %collective-permute-start.10 = (bf16[448,1024]{1,0:T(8,128)(2,1)}, bf16[448,1024]{1,0:T(8,128)(2,1)}, u32[]{:S(2)}, u32[]{:S(2)}) collective-permute-start(bf16[448,1024]{1,0:T(8,128)(2,1)} %bitcast.15.da0_ref), channel_id=1, source_target_pairs={{0,16},{16,0},{1,17},{17,1},{2,18},{18,2},{3,19},{19,3},{4,20},{20... | collective-permute-start | bytes 2752520 | tf_op jit(solution)/shard_map/ppermute | solution.py:151
  97.2 43.3 %collective-permute-start.12 = (bf16[448,1024]{1,0:T(8,128)(2,1)}, bf16[448,1024]{1,0:T(8,128)(2,1)S(1)}, u32[]{:S(2)}, u32[]{:S(2)}) collective-permute-start(bf16[448,1024]{1,0:T(8,128)(2,1)} %collective-permute-done.11.da1_ref), channel_id=1, source_target_pairs={{0,16},{16,0},{1,17},{17,1},{2,18},{18,2},{3,19},{19,3},{4,20},{20... | collective-permute-start | bytes 2752520 | tf_op jit(solution)/shard_map/ppermute | solution.py:155
  106.3 9.2 %collective-permute-start.3 = (bf16[256,256]{1,0:T(8,128)(2,1)S(1)}, bf16[256,256]{1,0:T(8,128)(2,1)S(1)}, u32[]{:S(2)}, u32[]{:S(2)}) collective-permute-start(bf16[256,256]{1,0:T(8,128)(2,1)S(1)} %gate_up.1.h0), channel_id=1, source_target_pairs={{0,2},{2,4},{4,6},{6,8},{8,10},{10,12},{12,14},{14,0},{1,3},{3,5},... | collective-permute-start | bytes 393224 | tf_op jit(solution)/shard_map/ppermute | solution.py:118
  110.4 11.8 %collective-permute-start.4 = (bf16[256,256]{1,0:T(8,128)(2,1)S(1)}, bf16[256,256]{1,0:T(8,128)(2,1)S(1)}, u32[]{:S(2)}, u32[]{:S(2)}) collective-permute-start(bf16[256,256]{1,0:T(8,128)(2,1)S(1)} %gate_up.1.h0), channel_id=1, source_target_pairs={{0,14},{2,0},{4,2},{6,4},{8,6},{10,8},{12,10},{14,12},{1,15},{3,1}... | collective-permute-start | bytes 393224 | tf_op jit(solution)/shard_map/ppermute | solution.py:121
  115.5 10.2 %collective-permute-start.5 = (bf16[256,256]{1,0:T(8,128)(2,1)S(1)}, bf16[256,256]{1,0:T(8,128)(2,1)S(1)}, u32[]{:S(2)}, u32[]{:S(2)}) collective-permute-start(bf16[256,256]{1,0:T(8,128)(2,1)S(1)} %collective-permute-done.3.h1), channel_id=1, source_target_pairs={{0,2},{2,4},{4,6},{6,8},{8,10},{10,12},{12,14},{14,0},{1,3},{3,5},... | collective-permute-start | bytes 393224 | tf_op jit(solution)/shard_map/ppermute | solution.py:118
  122.2 11.8 %collective-permute-start.6 = (bf16[256,256]{1,0:T(8,128)(2,1)S(1)}, bf16[256,256]{1,0:T(8,128)(2,1)S(1)}, u32[]{:S(2)}, u32[]{:S(2)}) collective-permute-start(bf16[256,256]{1,0:T(8,128)(2,1)S(1)} %collective-permute-done.4.h2), channel_id=1, source_target_pairs={{0,14},{2,0},{4,2},{6,4},{8,6},{10,8},{12,10},{14,12},{1,15},{3,1}... | collective-permute-start | bytes 393224 | tf_op jit(solution)/shard_map/ppermute | solution.py:121
  125.7 11.8 %collective-permute-start.7 = (bf16[256,256]{1,0:T(8,128)(2,1)S(1)}, bf16[256,256]{1,0:T(8,128)(2,1)S(1)}, u32[]{:S(2)}, u32[]{:S(2)}) collective-permute-start(bf16[256,256]{1,0:T(8,128)(2,1)S(1)} %collective-permute-done.5.h3), channel_id=1, source_target_pairs={{0,2},{2,4},{4,6},{6,8},{8,10},{10,12},{12,14},{14,0},{1,3},{3,5},... | collective-permute-start | bytes 393224 | tf_op jit(solution)/shard_map/ppermute | solution.py:118
  134.0 9.8 %collective-permute-start.8 = (bf16[256,256]{1,0:T(8,128)(2,1)S(1)}, bf16[256,256]{1,0:T(8,128)(2,1)S(1)}, u32[]{:S(2)}, u32[]{:S(2)}) collective-permute-start(bf16[256,256]{1,0:T(8,128)(2,1)S(1)} %collective-permute-done.6.h4), channel_id=1, source_target_pairs={{0,14},{2,0},{4,2},{6,4},{8,6},{10,8},{12,10},{14,12},{1,15},{3,1}... | collective-permute-start | bytes 393224 | tf_op jit(solution)/shard_map/ppermute | solution.py:121
  137.5 11.7 %collective-permute-start.9 = (bf16[256,256]{1,0:T(8,128)(2,1)S(1)}, bf16[256,256]{1,0:T(8,128)(2,1)S(1)}, u32[]{:S(2)}, u32[]{:S(2)}) collective-permute-start(bf16[256,256]{1,0:T(8,128)(2,1)S(1)} %collective-permute-done.7.h5), channel_id=1, source_target_pairs={{0,2},{2,4},{4,6},{6,8},{8,10},{10,12},{12,14},{14,0},{1,3},{3,5},... | collective-permute-start | bytes 393224 | tf_op jit(solution)/shard_map/ppermute | solution.py:118
